TPU v7x, 32 devices: a whole 2x2x4 slice. The times are simulated.
32 devices in a mesh: seq: 32 (over z, y, x, core).
Axes of the slice: x: 2, y: 2, z: 4, core: 2. Of those that a mesh axis runs over, the one named last changes fastest.
Arguments:
- tokens: bfloat16 [2, 8192, 1024], P(None, 'seq'), may hold values from -6 to 6
- ln1_gain: bfloat16 [1024], P('seq'), may hold values from 0.5 to 1.5
- ln1_bias: bfloat16 [1024], P('seq'), may hold values from -1.75 to 1.75
- qkv_weight: bfloat16 [1024, 3072], P('seq'), may hold values from -0.1875 to 0.1875
- q_bias: bfloat16 [1024], P('seq'), may hold values from -1.75 to 1.75
- v_bias: bfloat16 [1024], P('seq'), may hold values from -1.75 to 1.75
- out_weight: bfloat16 [1024, 1024], P('seq'), may hold values from -4 to 4
- out_bias: bfloat16 [1024], P('seq'), may hold values from -1.75 to 1.75
- ln2_gain: bfloat16 [1024], P('seq'), may hold values from 0.5 to 1.5
- ln2_bias: bfloat16 [1024], P('seq'), may hold values from -1.75 to 1.75
- fc1_weight: bfloat16 [1024, 4096], P('seq'), may hold values from -0.1875 to 0.1875
- fc1_bias: bfloat16 [4096], P('seq'), may hold values from -3 to 3
- fc2_weight: bfloat16 [4096, 1024], P('seq'), may hold values from -0.125 to 0.125
- fc2_bias: bfloat16 [1024], P('seq'), may hold values from -1.75 to 1.75
- image_ids: int32 [2, 8192], P(None, 'seq'), may hold values from 0 to 14, as said below
- image_starts: int32 [2, 15], replicated, may hold values from 0 to 8191, as said below
- cotangent: bfloat16 [2, 8192, 1024], P(None, 'seq'), may hold values from -6 to 6
Outputs:
- out: bfloat16 [2, 8192, 1024], P(None, 'seq')
- input_grad: bfloat16 [2, 8192, 1024], P(None, 'seq')
- ln1_gain_grad: float32 [1024], P('seq')
- ln1_bias_grad: float32 [1024], P('seq')
- qkv_weight_grad: float32 [1024, 3072], P('seq')
- q_bias_grad: float32 [1024], P('seq')
- v_bias_grad: float32 [1024], P('seq')
- out_weight_grad: float32 [1024, 1024], P('seq')
- out_bias_grad: float32 [1024], P('seq')
- ln2_gain_grad: float32 [1024], P('seq')
- ln2_bias_grad: float32 [1024], P('seq')
- fc1_weight_grad: float32 [1024, 4096], P('seq')
- fc1_bias_grad: float32 [4096], P('seq')
- fc2_weight_grad: float32 [4096, 1024], P('seq')
- fc2_bias_grad: float32 [1024], P('seq')
Inputs may be any that keep to these rules, and one draw needn't show every extreme that they name: In micro-batch m the images are contiguous runs in order: image i covers positions image_starts[m, i] to image_starts[m, i + 1] - 1 (the last one to 8191) and image_ids[m, t] names the image of position t; every image has exactly 577 tokens except one padding run, at a place drawn from the seed, of 8192 % 577 tokens. image_starts[m, 0] = 0 and the starts rise strictly; every start is a position of the stream.
All inputs are finite; a program needn't handle non-finite values.
Results may differ from a plain program's by a relative error of at most 0.013.
Values may be sent and summed in bfloat16 or wider, within the bound.
No kernel may reach another device: no remote copies, remote signals or barrier semaphores. Data moves between devices by JAX's collectives and lax.ppermute only.
A program may use at most 256 MiB of HBM per device.

v0:
```python
import functools

import jax
import jax.numpy as jnp
from jax import lax
from jax.experimental import pallas as pl
from jax.experimental.pallas import tpu as pltpu
from jax.sharding import PartitionSpec as P

HEAD_DIM = 64
IMG_TOK = 577
PLANE = 8
PAIR = 2 * HEAD_DIM
HALO = IMG_TOK - 1
LEAD = 640
WINDOW = 640
TILE = 256

epsilon = 1e-05
negative_fill = -1e30
bf16 = jnp.bfloat16
f32 = jnp.float32


def product(left, right):
    return jnp.dot(left, right, preferred_element_type=f32)


def product_tn(left, right):
    return lax.dot_general(left, right, (((0,), (0,)), ((), ())), preferred_element_type=f32)


def product_nt(left, right):
    return lax.dot_general(left, right, (((1,), (1,)), ((), ())), preferred_element_type=f32)


def swap(block, bit):
    n = lax.axis_size("seq")
    return lax.ppermute(block, "seq", [(i, i ^ bit) for i in range(n)])


def shift_plane(block, planes):
    n = lax.axis_size("seq")
    step = planes * PLANE
    return lax.ppermute(block, "seq", [(i, i + step) for i in range(n) if 0 <= i + step < n])


def places(order):
    held = [0]
    for bit in order:
        held = held + [r ^ bit for r in held]
    return held


def gather_bits(block, order):
    current = block[None]
    for bit in order[:-1]:
        current = jnp.concatenate([current, swap(current, bit)], axis=0)
    return current, swap(current, order[-1])


def position(r, order):
    return sum(((r >> (bit.bit_length() - 1)) & 1) << k for k, bit in enumerate(order))


def tie(value, *earlier):
    return lax.optimization_barrier((value,) + earlier)[0]


def own_bit(me, bit):
    return jnp.where(jnp.bitwise_and(me, bit) != 0, 1, 0)


def pick(block, axis, index):
    return lax.dynamic_index_in_dim(block, index, axis, keepdims=False)


def exchange(blocks):
    bits = PLANE.bit_length() - 1
    cube = blocks.reshape((2,) * bits + blocks.shape[1:])
    for axis in reversed(range(bits)):
        got = swap(lax.index_in_dim(cube, 1, axis, keepdims=False), 1 << (bits - 1 - axis))
        cube = jnp.stack([lax.index_in_dim(cube, 0, axis, keepdims=False), got], axis=axis)
    return cube.reshape(blocks.shape)


class Scatter:
    def __init__(self, me, partials, order):
        self.me = me
        self.partials = partials
        depth = sum(item.shape[0] for item in partials[0]).bit_length() - 1
        self.bits = [1 << (depth - 1 - axis) for axis in range(depth)]
        self.order = list(order)
        self.split()

    def half(self, axis, index):
        if self.partials is None:
            kept = pick(self.block, axis, index).astype(f32)
            return (kept + pick(self.got, axis, index).astype(f32)).astype(bf16)
        joined = []
        for items in self.partials:
            picked = [pick(item.reshape((-1, 2) + item.shape[1:]), 1, index) for item in items]
            joined.append(picked[0] if len(picked) == 1 else jnp.concatenate(picked, axis=0))
        joined = joined[0] if len(joined) == 1 else jnp.concatenate(joined, axis=1)
        return joined.reshape((2,) * len(self.bits) + joined.shape[1:])

    def split(self):
        self.bit = self.order.pop(0)
        axis = self.bits.index(self.bit)
        self.bits.pop(axis)
        mine = own_bit(self.me, self.bit)
        self.send, keep = self.half(axis, 1 - mine), self.half(axis, mine)
        self.block, self.got, self.partials = keep, None, None

    def swap(self):
        self.got = swap(self.send, self.bit)

    def advance(self, *earlier):
        if earlier:
            self.got = tie(self.got, *earlier)
        self.split()
        self.swap()

    def total(self):
        return self.block.astype(f32) + self.got.astype(f32)


def turn_kernel(info, blocks, turned):
    for r in range(blocks.shape[0]):
        turned[r] = blocks[jnp.bitwise_xor(info[0], r)]


def turn_blocks(info, blocks):
    return pl.pallas_call(
        turn_kernel,
        grid_spec=pltpu.PrefetchScalarGridSpec(
            num_scalar_prefetch=1,
            grid=(1,),
            in_specs=[pl.BlockSpec(blocks.shape, lambda g, i: (0, 0, 0))],
            out_specs=pl.BlockSpec(blocks.shape, lambda g, i: (0, 0, 0)),
        ),
        out_shape=jax.ShapeDtypeStruct(blocks.shape, blocks.dtype),
    )(info, blocks)


def load_rows(orders, micros, place_in_plane, qkv, before, after, queries, keys, values, sem):
    blocks, rows = qkv.shape[1], qkv.shape[2]
    own = blocks * rows
    for buffer in (keys, values):
        for slot in range(len(micros)):
            buffer[slot, 0 : LEAD - HALO, :] = jnp.zeros((LEAD - HALO, PAIR), bf16)
            tail = buffer.shape[1] - (LEAD + own + HALO)
            buffer[slot, LEAD + own + HALO :, :] = jnp.zeros((tail, PAIR), bf16)
    started = []
    for slot, m in enumerate(micros):
        for p, r in enumerate(places(orders[m])):
            spot = pl.multiple_of(jnp.bitwise_xor(place_in_plane, r) * rows, rows)
            started += [
                pltpu.make_async_copy(
                    qkv.at[m, p, :, pl.ds(0, PAIR)], queries.at[slot, pl.ds(spot, rows)], sem
                ),
                pltpu.make_async_copy(
                    qkv.at[m, p, :, pl.ds(PAIR, PAIR)], keys.at[slot, pl.ds(LEAD + spot, rows)], sem
                ),
                pltpu.make_async_copy(
                    qkv.at[m, p, :, pl.ds(2 * PAIR, PAIR)], values.at[slot, pl.ds(LEAD + spot, rows)], sem
                ),
            ]
        for which, buffer in enumerate((keys, values)):
            columns = pl.ds(which * PAIR, PAIR)
            started += [
                pltpu.make_async_copy(
                    before.at[m, :, columns], buffer.at[slot, pl.ds(LEAD - HALO, HALO)], sem
                ),
                pltpu.make_async_copy(
                    after.at[m, :, columns], buffer.at[slot, pl.ds(LEAD + own, HALO)], sem
                ),
            ]
    return started


def image_span(bounds, m, image, base):
    begin = bounds[m, image] - base + LEAD
    finish = bounds[m, image + 1] - base + LEAD
    return begin, finish


def key_block(keys, m, begin, finish, key_start, key_aug):
    key_aug[:, :PAIR] = keys[m, pl.ds(key_start, WINDOW), :]
    rows = key_start + lax.broadcasted_iota(jnp.int32, (WINDOW, PAIR), 0)
    inside = (rows >= begin) & (rows < finish)
    key_aug[:, PAIR:] = jnp.where(inside, 0.0, negative_fill).astype(bf16)


def split_heads(rows_f32, lanes):
    first = jnp.where(lanes < HEAD_DIM, rows_f32, 0.0).astype(bf16)
    second = jnp.where(lanes >= HEAD_DIM, rows_f32, 0.0).astype(bf16)
    return first, second


def attend_kernel(
    orders, info, bounds, qkv, before, after, mixed, stats, queries, keys, values, result, result_low, key_aug, value_t, sem
):
    micro_count, blocks, rows, _ = qkv.shape
    own = blocks * rows
    place_in_plane, base = info[1], info[2]
    image_count = bounds.shape[1] - 1
    started = load_rows(orders, range(micro_count), place_in_plane, qkv, before, after, queries, keys, values, sem)
    for copy in started:
        copy.start()
    value_t[:, HEAD_DIM:, :] = jnp.ones((2, 16, WINDOW), bf16)
    lanes = lax.broadcasted_iota(jnp.int32, (TILE, PAIR), 1)
    rows_iota = lax.broadcasted_iota(jnp.int32, (TILE, PAIR), 0)
    lane_row = lax.broadcasted_iota(jnp.int32, (1, TILE), 1)
    query_mark = jnp.where(lanes == 0, 1.0, 0.0).astype(bf16)
    for copy in started:
        copy.wait()

    for m in range(micro_count):

        def one_image(image, carry):
            begin, finish = image_span(bounds, m, image, base)

            @pl.when((finish > LEAD) & (begin < LEAD + own))
            def _():
                key_start = pl.multiple_of((begin >> 4) << 4, 16)
                key_block(keys, m, begin, finish, key_start, key_aug)
                turned = values[m, pl.ds(key_start, WINDOW), :].astype(f32).T
                value_t[0, :HEAD_DIM, :] = turned[:HEAD_DIM].astype(bf16)
                value_t[1, :HEAD_DIM, :] = turned[HEAD_DIM:].astype(bf16)
                first_tile = jnp.maximum(begin - LEAD, 0) >> 8
                last_tile = (jnp.minimum(finish - LEAD, own) + TILE - 1) >> 8

                def one_tile(tile, carry):
                    spot = pl.multiple_of(tile * TILE, TILE)
                    scaled = queries[m, pl.ds(spot, TILE), :].astype(f32) * (HEAD_DIM**-0.5)
                    pieces = []
                    inside_lane = (lane_row + (spot + LEAD) >= begin) & (lane_row + (spot + LEAD) < finish)
                    for h, query in enumerate(split_heads(scaled, lanes)):
                        aug = jnp.concatenate([query, query_mark], axis=1)
                        scores = product_nt(key_aug[...], aug)
                        peak = jnp.max(scores, axis=0, keepdims=True)
                        weights = jnp.exp(scores - peak).astype(bf16)
                        out = product(value_t[h], weights)
                        total = out[HEAD_DIM : HEAD_DIM + 1]
                        pieces.append(out[:HEAD_DIM] / total)
                        row = (m * 2 + h) * blocks + tile
                        stats[pl.ds(row, 1), :] = jnp.where(
                            inside_lane, peak + jnp.log(total), stats[pl.ds(row, 1), :]
                        )
                    value = jnp.concatenate(pieces, axis=0).T
                    place_row = rows_iota + (spot + LEAD)
                    inside = (place_row >= begin) & (place_row < finish)
                    result[m, pl.ds(spot, TILE), :] = jnp.where(
                        inside, value, result[m, pl.ds(spot, TILE), :]
                    )
                    return carry

                lax.fori_loop(first_tile, last_tile, one_tile, 0)

            return carry

        lax.fori_loop(0, image_count, one_image, 0)

    result_low[...] = result[...].astype(bf16)
    started = []
    for m in range(micro_count):
        for r in range(blocks):
            spot = pl.multiple_of(jnp.bitwise_xor(place_in_plane, r) * rows, rows)
            started.append(pltpu.make_async_copy(result_low.at[m, pl.ds(spot, rows)], mixed.at[r, m], sem))
    for copy in started:
        copy.start()
    for copy in started:
        copy.wait()


def attend_back_kernel(m, orders, info, bounds, qkv, before, after, mixed, *refs):
    blocks, rows = qkv.shape[1], qkv.shape[2]
    own = blocks * rows
    grad_mixed, refs = refs[:blocks], refs[blocks:]
    stats, grad_query, grad_pairs, grad_before, grad_after, refs = *refs[:5], refs[5:]
    queries, keys, values, result, grads, key_aug, key_t, acc_query, acc_key, acc_value, edge, sem = refs
    place_in_plane, base = info[1], info[2]
    image_count = bounds.shape[1] - 1
    started = load_rows(orders, [m], place_in_plane, qkv, before, after, queries, keys, values, sem)
    for r in range(blocks):
        spot = pl.multiple_of(jnp.bitwise_xor(place_in_plane, r) * rows, rows)
        started += [
            pltpu.make_async_copy(mixed.at[r, m], result.at[pl.ds(spot, rows)], sem),
            pltpu.make_async_copy(grad_mixed[r].at[m], grads.at[pl.ds(spot, rows)], sem),
        ]
    for copy in started:
        copy.start()
    acc_query[...] = jnp.zeros_like(acc_query)
    acc_key[...] = jnp.zeros_like(acc_key)
    acc_value[...] = jnp.zeros_like(acc_value)
    lanes = lax.broadcasted_iota(jnp.int32, (TILE, PAIR), 1)
    lane_row = lax.broadcasted_iota(jnp.int32, (1, TILE), 1)
    query_mark = jnp.where(lanes == 0, 1.0, 0.0).astype(bf16)
    for copy in started:
        copy.wait()


    def one_image(image, carry):
        begin, finish = image_span(bounds, m, image, base)

        @pl.when((finish > LEAD) & (begin < LEAD + own))
        def _():
            key_start = pl.multiple_of((begin >> 4) << 4, 16)
            key_rows = pl.ds(key_start, WINDOW)
            key_block(keys, 0, begin, finish, key_start, key_aug)
            turned = keys[0, key_rows, :].astype(f32).T
            key_t[0] = turned[:HEAD_DIM].astype(bf16)
            key_t[1] = turned[HEAD_DIM:].astype(bf16)
            first_tile = jnp.maximum(begin - LEAD, 0) >> 8
            last_tile = (jnp.minimum(finish - LEAD, own) + TILE - 1) >> 8

            def one_tile(tile, carry):
                spot = pl.multiple_of(tile * TILE, TILE)
                here = pl.ds(spot, TILE)
                scaled = queries[0, here, :].astype(f32) * (HEAD_DIM**-0.5)
                grad = grads[ here, :].astype(f32)
                dots = (grad * result[ here, :].astype(f32)).T
                inside_lane = (lane_row + (spot + LEAD) >= begin) & (lane_row + (spot + LEAD) < finish)
                both = zip(split_heads(scaled, lanes), split_heads(grad, lanes))
                pieces = []
                add_key, add_value = None, None
                for h, (query, grad_h) in enumerate(both):
                    row = (m * 2 + h) * blocks + tile
                    level = jnp.where(inside_lane, stats[pl.ds(row, 1), :], -negative_fill)
                    row_dot = jnp.sum(
                        dots[h * HEAD_DIM : (h + 1) * HEAD_DIM], axis=0, keepdims=True
                    )
                    aug = jnp.concatenate([query, query_mark], axis=1)
                    shares = jnp.exp(product_nt(key_aug[...], aug) - level)
                    grad_share = product_nt(values[0, key_rows, :], grad_h)
                    grad_scores = (shares * (grad_share - row_dot)).astype(bf16)
                    value_part = product(shares.astype(bf16), grad_h)
                    key_part = product(grad_scores, query)
                    add_value = value_part if h == 0 else add_value + value_part
                    add_key = key_part if h == 0 else add_key + key_part
                    pieces.append(product(key_t[h], grad_scores))
                acc_value[ key_rows, :] += add_value
                acc_key[ key_rows, :] += add_key
                acc_query[ here, :] += jnp.concatenate(pieces, axis=0).T * (HEAD_DIM**-0.5)
                return carry

            lax.fori_loop(first_tile, last_tile, one_tile, 0)

        return carry

    lax.fori_loop(0, image_count, one_image, 0)

    edge_rows = grad_before.shape[0]
    edge[0, : edge_rows - HALO, :] = jnp.zeros((edge_rows - HALO, 2 * PAIR), bf16)
    edge[1, HALO:, :] = jnp.zeros((edge_rows - HALO, 2 * PAIR), bf16)
    started = [pltpu.make_async_copy(acc_query, grad_query, sem)]
    for which, acc in enumerate((acc_key, acc_value)):
        columns = pl.ds(which * PAIR, PAIR)
        edge[0, edge_rows - HALO :, which * PAIR : (which + 1) * PAIR] = acc[LEAD - HALO : LEAD, :].astype(bf16)
        edge[1, :HALO, which * PAIR : (which + 1) * PAIR] = acc[LEAD + own : LEAD + own + HALO, :].astype(bf16)
        started.append(pltpu.make_async_copy(acc.at[pl.ds(LEAD, own)], grad_pairs.at[:, columns], sem))
    started.append(pltpu.make_async_copy(edge.at[0], grad_before, sem))
    started.append(pltpu.make_async_copy(edge.at[1], grad_after, sem))
    for copy in started:
        copy.start()
    for copy in started:
        copy.wait()


def cover(rows, passes):
    scores = 2 * rows * WINDOW
    return pl.CostEstimate(
        flops=4 * scores * PAIR, transcendentals=scores, bytes_accessed=passes * scores
    )


def any_specs(count):
    return [pl.BlockSpec(memory_space=pl.ANY)] * count


def attend(orders, info, bounds, qkv, before, after):
    micro_count, blocks, rows, _ = qkv.shape
    own = blocks * rows
    span = LEAD + own + LEAD
    stat_rows = micro_count * 2 * blocks
    return pl.pallas_call(
        functools.partial(attend_kernel, orders),
        grid_spec=pltpu.PrefetchScalarGridSpec(
            num_scalar_prefetch=2,
            grid=(1,),
            in_specs=any_specs(3),
            out_specs=any_specs(1) + [pl.BlockSpec((stat_rows, TILE), lambda g, a, b: (0, 0))],
            scratch_shapes=[
                pltpu.VMEM((micro_count, own, PAIR), bf16),
                pltpu.VMEM((micro_count, span, PAIR), bf16),
                pltpu.VMEM((micro_count, span, PAIR), bf16),
                pltpu.VMEM((micro_count, own, PAIR), f32),
                pltpu.VMEM((micro_count, own, PAIR), bf16),
                pltpu.VMEM((WINDOW, 2 * PAIR), bf16),
                pltpu.VMEM((2, HEAD_DIM + 16, WINDOW), bf16),
                pltpu.SemaphoreType.DMA,
            ],
        ),
        out_shape=[
            jax.ShapeDtypeStruct((blocks, micro_count, rows, PAIR), bf16),
            jax.ShapeDtypeStruct((stat_rows, TILE), f32),
        ],
        cost_estimate=cover(micro_count * own, 30),
    )(info, bounds, qkv, before, after)


def attend_back(m, orders, info, bounds, qkv, before, after, mixed, grad_mixed, stats):
    _, blocks, rows, _ = qkv.shape
    own = blocks * rows
    span = LEAD + own + LEAD
    edge_rows = -(-HALO // rows) * rows
    return pl.pallas_call(
        functools.partial(attend_back_kernel, m, orders),
        grid_spec=pltpu.PrefetchScalarGridSpec(
            num_scalar_prefetch=2,
            grid=(1,),
            in_specs=any_specs(4 + blocks) + [pl.BlockSpec(stats.shape, lambda g, a, b: (0, 0))],
            out_specs=any_specs(4),
            scratch_shapes=[
                pltpu.VMEM((1, own, PAIR), bf16),
                pltpu.VMEM((1, span, PAIR), bf16),
                pltpu.VMEM((1, span, PAIR), bf16),
                pltpu.VMEM((own, PAIR), bf16),
                pltpu.VMEM((own, PAIR), bf16),
                pltpu.VMEM((WINDOW, 2 * PAIR), bf16),
                pltpu.VMEM((2, HEAD_DIM, WINDOW), bf16),
                pltpu.VMEM((own, PAIR), f32),
                pltpu.VMEM((span, PAIR), f32),
                pltpu.VMEM((span, PAIR), f32),
                pltpu.VMEM((2, edge_rows, 2 * PAIR), bf16),
                pltpu.SemaphoreType.DMA,
            ],
        ),
        out_shape=[
            jax.ShapeDtypeStruct((own, PAIR), f32),
            jax.ShapeDtypeStruct((own, 2 * PAIR), f32),
            jax.ShapeDtypeStruct((edge_rows, 2 * PAIR), bf16),
            jax.ShapeDtypeStruct((edge_rows, 2 * PAIR), bf16),
        ],
        cost_estimate=cover(own, 35),
    )(info, bounds, qkv, before, after, mixed, *grad_mixed, stats)


def join_kernel(order, info, query, pairs, head, tail, joined):
    blocks, rows, _ = joined.shape
    edge_blocks = head.shape[0] // rows
    for tile in range(blocks):
        here = pl.ds(tile * rows, rows)
        total = pairs[here, :]
        if tile < edge_blocks:
            total = total + head[here, :].astype(f32)
        if tile >= blocks - edge_blocks:
            total = total + tail[pl.ds((tile - (blocks - edge_blocks)) * rows, rows), :].astype(f32)
        target = position(jnp.bitwise_xor(info[1], tile), order)
        joined[target, :, :PAIR] = query[here, :].astype(bf16)
        joined[target, :, PAIR:] = total.astype(bf16)


def join_grads(order, info, grad_query, grad_pairs, head, tail, rows):
    own = grad_query.shape[0]
    blocks = own // rows
    ins = (grad_query, grad_pairs, head, tail)
    return pl.pallas_call(
        functools.partial(join_kernel, order),
        grid_spec=pltpu.PrefetchScalarGridSpec(
            num_scalar_prefetch=1,
            grid=(1,),
            in_specs=[pl.BlockSpec(item.shape, lambda g, i: (0, 0)) for item in ins],
            out_specs=pl.BlockSpec((blocks, rows, 3 * PAIR), lambda g, i: (0, 0, 0)),
        ),
        out_shape=jax.ShapeDtypeStruct((blocks, rows, 3 * PAIR), bf16),
    )(info, *ins)


def layer_norm_parts(values, gain, shift):
    center = values - jnp.mean(values, axis=-1, keepdims=True)
    inverse = lax.rsqrt(jnp.mean(center * center, axis=-1, keepdims=True) + epsilon)
    normal = center * inverse
    return (normal * gain + shift, normal, inverse)


def layer_norm_back(grad_normed, normal, inverse, gain):
    scaled = grad_normed * gain
    centered = scaled - jnp.mean(scaled, axis=-1, keepdims=True)
    return inverse * (centered - normal * jnp.mean(scaled * normal, axis=-1, keepdims=True))


class PlaneScatter:
    def __init__(self, partial, held, order):
        self.pieces = [partial[position(r, held)].astype(bf16) for r in range(PLANE)]
        self.left = list(range(PLANE))
        self.order = list(order)

    def start(self, *earlier):
        self.bit = self.order.pop(0)
        self.keep = [r for r in self.left if not r & self.bit]
        self.send = jnp.stack([self.pieces[r | self.bit] for r in self.keep])
        if earlier:
            self.send = tie(self.send, *earlier)
        self.got = swap(self.send, self.bit)

    def finish(self):
        for position, r in enumerate(self.keep):
            added = self.pieces[r].astype(f32) + self.got[position].astype(f32)
            self.pieces[r] = added.astype(bf16) if self.order else added
        self.left = self.keep


def body(
    tokens,
    ln1_gain,
    ln1_bias,
    qkv_weight,
    q_bias,
    v_bias,
    out_weight,
    out_bias,
    ln2_gain,
    ln2_bias,
    fc1_weight,
    fc1_bias,
    fc2_weight,
    fc2_bias,
    image_ids,
    image_starts,
    cotangent,
):
    micro_count, tok_dev, model_width = tokens.shape
    n = lax.axis_size("seq")
    own_tokens = micro_count * tok_dev
    plane_rows = PLANE * tok_dev
    stream_len = tok_dev * n
    me = lax.axis_index("seq")
    mine = jnp.bitwise_and(me, PLANE - 1)
    base = (me - mine) * tok_dev
    info = jnp.stack([me, mine, base]).astype(jnp.int32)
    bounds = jnp.concatenate(
        [image_starts, jnp.full((micro_count, 1), stream_len, jnp.int32)], axis=1
    )
    plane_bits = [1, 2, 4]
    depth_bits = []
    bit = PLANE
    while bit < n:
        depth_bits.append(bit)
        bit *= 2

    small = [ln1_gain, ln1_bias, q_bias, v_bias, out_bias, ln2_gain, ln2_bias, fc2_bias, fc1_bias]
    shard_rows = qkv_weight.shape[0]
    small_len = sum(item.shape[0] for item in small)
    spare_rows = -(-small_len // (8 * 3 * PAIR)) * 8
    narrow = small[0].shape[0]
    small_rows = jnp.concatenate([item.reshape(-1, narrow) for item in small], axis=0)
    used = small_rows.shape[0]
    small_rows = jnp.pad(small_rows, ((0, -used % 16), (0, 3 * PAIR - narrow)))
    by_pair = qkv_weight.reshape(shard_rows, 3, PLANE, PAIR).transpose(2, 0, 1, 3)
    by_pair = by_pair.reshape(PLANE, shard_rows, 3 * PAIR)
    outgoing = jnp.concatenate(
        [by_pair, jnp.broadcast_to(small_rows[None], (PLANE,) + small_rows.shape)], axis=1
    )
    arrived = exchange(outgoing[jnp.bitwise_xor(mine, jnp.arange(PLANE))])

    token_orders = [[2, 4, 1] if m % 2 == 0 else [4, 2, 1] for m in range(micro_count)]
    gathered = [tokens[m][None] for m in range(micro_count)]
    current = arrived
    for k in range(3):
        got = [swap(item, token_orders[m][k]) for m, item in enumerate(gathered)]
        if k == 1:
            current = current[None]
            for bit in depth_bits[::-1]:
                current = jnp.stack([current, swap(current, bit)], axis=1)
                current = current.reshape((-1,) + arrived.shape)
            current = current.reshape((n,) + arrived.shape[1:])
            early = got + [current]
            got[0] = tie(got[0], current)
        gathered = [jnp.concatenate(pair, axis=0) for pair in zip(gathered, got)]

    step = out_weight.shape[0]
    wide_parts = fc1_weight.shape[1] // model_width
    shards = [out_weight]
    shards += [fc1_weight[:, k * model_width : (k + 1) * model_width] for k in range(wide_parts)]
    packed = tie(jnp.concatenate(shards + [fc2_weight], axis=0), *early)
    every = lax.all_gather(packed, "seq")
    out_full = every[:, :step].reshape(model_width, model_width)
    ups = [every[:, (1 + k) * step : (2 + k) * step].reshape(model_width, -1) for k in range(wide_parts)]
    share = n // wide_parts
    downs = [
        every[k * share : (k + 1) * share, (1 + wide_parts) * step :].reshape(-1, model_width)
        for k in range(wide_parts)
    ]

    pair_blocks = turn_blocks(info, current)
    pair_weight = pair_blocks[:, :shard_rows].reshape(n * shard_rows, 3 * PAIR)
    small_all = pair_blocks[:, shard_rows : shard_rows + used, :narrow].astype(f32)
    small_full = [small_all[:, k].reshape(-1) for k in range(len(small) - 1)]
    small_full.append(small_all[:, len(small) - 1 :].reshape(-1))
    gain_one, shift_one, q_shift, v_shift, out_shift, gain_two, shift_two, down_shift, up_shift = small_full

    plane_stream = jnp.stack(gathered)
    plane_flat = plane_stream.reshape(micro_count * plane_rows, model_width)
    normed, _, _ = layer_norm_parts(plane_flat.astype(f32), gain_one, shift_one)
    normed_low = normed.astype(bf16)
    pair_shift = jnp.concatenate(
        [
            lax.dynamic_slice_in_dim(q_shift, mine * PAIR, PAIR),
            jnp.zeros((PAIR,), f32),
            lax.dynamic_slice_in_dim(v_shift, mine * PAIR, PAIR),
        ]
    )
    qkv = (product(normed_low, pair_weight) + pair_shift).astype(bf16)
    qkv = qkv.reshape(micro_count, PLANE, tok_dev, 3 * PAIR)

    edge_blocks = -(-HALO // tok_dev)

    def plane_block(index):
        offset = jnp.bitwise_xor(mine, index)
        blocks = [pick(qkv[m], 0, position(offset, order)) for m, order in enumerate(token_orders)]
        return jnp.stack(blocks)[:, :, PAIR:]

    last_rows = jnp.concatenate([plane_block(PLANE - edge_blocks + k) for k in range(edge_blocks)], axis=1)
    first_rows = jnp.concatenate([plane_block(k) for k in range(edge_blocks)], axis=1)
    before = shift_plane(last_rows[:, edge_blocks * tok_dev - HALO :], 1)
    after = shift_plane(first_rows[:, :HALO], -1)
    mixed_pair, stats = attend(token_orders, info, bounds, qkv, before, after)

    def column(r):
        return jnp.bitwise_xor(mine, r) * PAIR

    mixed_low = jnp.zeros((own_tokens, model_width), bf16)
    for r in range(PLANE):
        part = mixed_pair[r] if r == 0 else swap(mixed_pair[r], r)
        mixed_low = lax.dynamic_update_slice(mixed_low, part.reshape(own_tokens, PAIR), (0, column(r)))

    stream = tokens.reshape(own_tokens, model_width).astype(f32)
    cotangent_low = cotangent.reshape(own_tokens, model_width)
    middle = stream + product(mixed_low, out_full) + out_shift
    normed_two, normal_two, inverse_two = layer_norm_parts(middle, gain_two, shift_two)
    normed_two_low = normed_two.astype(bf16)
    up_shifts = up_shift.reshape(wide_parts, model_width)
    actives, grad_hiddens = [], []
    for k in range(wide_parts):
        hidden = product(normed_two_low, ups[k]) + up_shifts[k]
        gate = jax.nn.sigmoid(1.702 * hidden)
        actives.append((hidden * gate).astype(bf16))
        grad_active = product_nt(cotangent_low, downs[k])
        grad_hiddens.append((grad_active * (gate + 1.702 * hidden * gate * (1.0 - gate))).astype(bf16))

    def by_device(partial, devices=n):
        return partial.astype(bf16).reshape(devices, -1, model_width)

    order_a = [1, 2, 4] + depth_bits
    order_b = [1, 4, 2] + depth_bits
    grad_downs = [by_device(product_tn(active, cotangent_low), share) for active in actives]
    half = grad_downs[0].shape[1] // 2
    down = [
        Scatter(me, [[item[:, :half] for item in grad_downs]], [1] + depth_bits[:1] + [2, 4] + depth_bits[1:]),
        Scatter(me, [[item[:, half:] for item in grad_downs]], [1] + depth_bits[:1] + [4, 2] + depth_bits[1:]),
    ]
    for part in down:
        part.swap()
    grad_hiddens[0] = tie(grad_hiddens[0], *[part.send for part in down])

    grad_normed_two = product_nt(grad_hiddens[0], ups[0])
    for k in range(1, wide_parts):
        grad_normed_two = grad_normed_two + product_nt(grad_hiddens[k], ups[k])
    for part in down:
        part.advance(grad_normed_two)
    grad_normed_two = tie(grad_normed_two, *[part.send for part in down])
    grad_middle = cotangent_low.astype(f32) + layer_norm_back(
        grad_normed_two, normal_two, inverse_two, gain_two
    )
    grad_branch_low = grad_middle.astype(bf16)
    grad_mixed_low = product_nt(grad_branch_low, out_full).astype(bf16)
    grad_parts = []
    for r in range(PLANE):
        part = lax.dynamic_slice(grad_mixed_low, (0, column(r)), (own_tokens, PAIR))
        part = part.reshape(micro_count, tok_dev, PAIR)
        grad_parts.append(part if r == 0 else swap(part, r))

    later = tie(normed_two_low, grad_mixed_low)
    grad_ups = [by_device(product_tn(later, grad_hidden)) for grad_hidden in grad_hiddens]
    grad_out_weight = by_device(product_tn(mixed_low, grad_branch_low))
    mid = wide_parts // 2
    up = [
        Scatter(me, [[item] for item in grad_ups[:mid] + [grad_out_weight[:, : step // 2]]], order_a),
        Scatter(me, [[item] for item in grad_ups[mid:] + [grad_out_weight[:, step // 2 :]]], order_b),
    ]
    for part in up:
        part.swap()
    result = middle + down_shift
    after_up = tie(actives[0], *[part.send for part in up])
    for k in range(wide_parts):
        result = result + product(after_up if k == 0 else actives[k], downs[k])
    result_low = result.astype(bf16)
    for part in up:
        part.advance(result_low, *grad_parts)

    before_back = [part.send for part in up]
    grad_planes = []
    grad_pair_weight, column_sum = 0.0, 0.0
    for m in range(micro_count):
        own_grad = tie(grad_parts[0], *before_back)
        grad_query, grad_pairs, grad_before, grad_after = attend_back(
            m, token_orders, info, bounds, qkv, before, after, mixed_pair, [own_grad] + grad_parts[1:], stats
        )
        from_next = shift_plane(grad_before, -1)
        from_last = shift_plane(grad_after, 1)
        for plane in grad_planes:
            plane.got = tie(plane.got, grad_before)
            plane.finish()
            plane.start()
        for part in up + down:
            part.advance(grad_before)
        sends = [part.send for part in up + down] + [plane.send for plane in grad_planes]
        grad_query = tie(grad_query, *sends)
        joined = join_grads(token_orders[m], info, grad_query, grad_pairs, from_last, from_next, tok_dev)
        grad_flat = joined.reshape(plane_rows, 3 * PAIR)
        grad_plane = product_nt(grad_flat, pair_weight).reshape(PLANE, tok_dev, model_width)
        order = [1, 2, 4] if m % 2 == 0 else [1, 4, 2]
        plane = PlaneScatter(grad_plane, token_orders[m], order)
        plane.start()
        grad_flat = tie(grad_flat, plane.send)
        rows = normed_low[m * plane_rows : (m + 1) * plane_rows]
        added = product_tn(rows, grad_flat)
        grad_pair_weight = grad_pair_weight + added
        column_sum = column_sum + jnp.sum(grad_flat.astype(f32), axis=0)
        if m < micro_count - 1:
            plane.got = tie(plane.got, added)
        plane.finish()
        plane.start()
        grad_planes.append(plane)
        before_back = [plane.send]
    grad_pair_weight = tie(grad_pair_weight, plane.send)

    wide = pair_weight.astype(f32)
    grad_shift_one = jnp.sum(wide * column_sum, axis=1)
    grad_gain_one = jnp.sum(wide * grad_pair_weight, axis=1)
    grad_gain_one = (grad_gain_one - shift_one * grad_shift_one) / gain_one

    def at_columns(part):
        return lax.dynamic_update_slice(jnp.zeros((model_width,), f32), part, (mine * PAIR,))

    small_grads = [
        grad_gain_one,
        grad_shift_one,
        at_columns(column_sum[:PAIR]),
        at_columns(column_sum[2 * PAIR :]),
        jnp.sum(grad_branch_low.astype(f32), axis=0),
        jnp.sum(grad_normed_two * normal_two, axis=0),
        jnp.sum(grad_normed_two, axis=0),
        jnp.sum(cotangent_low.astype(f32), axis=0),
        jnp.concatenate([jnp.sum(item.astype(f32), axis=0) for item in grad_hiddens]),
    ]
    small_out = jnp.concatenate([item.reshape(n, -1) for item in small_grads], axis=1).astype(bf16)
    small_out = jnp.pad(small_out, ((0, 0), (0, spare_rows * 3 * PAIR - small_len)))
    small_out = small_out.reshape(n, spare_rows, 3 * PAIR)
    leaving = jnp.concatenate(
        [grad_pair_weight.astype(bf16).reshape(n, shard_rows, 3 * PAIR), small_out], axis=1
    )
    turned = turn_blocks(info, leaving)

    turned = turned.reshape((n // PLANE, PLANE) + turned.shape[1:])
    for index, bit in enumerate(depth_bits):
        turned = turned.reshape((-1, 2) + turned.shape[1:])
        sent = turned[:, 1]
        got = swap(sent, bit)
        if index == 0:
            plane = grad_planes[-1]
            plane.got = tie(plane.got, sent)
            plane.finish()
            plane.start()
            for part in up + down:
                if part.order:
                    part.advance(sent, plane.send)
            got = tie(got, *[part.send for part in up + down])
        turned = (turned[:, 0].astype(f32) + got.astype(f32)).astype(bf16)
    turned = turned.reshape((PLANE,) + turned.shape[2:])
    for plane in grad_planes:
        plane.finish()
    grad_normed = jnp.concatenate([plane.pieces[0] for plane in grad_planes], axis=0)
    _, normal_one, inverse_one = layer_norm_parts(stream, gain_one, shift_one)
    grad_stream = grad_middle + layer_norm_back(grad_normed, normal_one, inverse_one, gain_one)
    stream_low = grad_stream.astype(bf16)
    for part in up + down:
        while part.order:
            part.advance(stream_low)
    down_sum = jnp.concatenate([part.total() for part in down], axis=0)
    up_totals = [part.total() for part in up]
    out_sum = jnp.concatenate([total[mid * step :] for total in up_totals], axis=0)
    up_sum = jnp.concatenate([total[: mid * step] for total in up_totals], axis=0)
    up_sum = jnp.concatenate([up_sum[k * step : (k + 1) * step] for k in range(wide_parts)], axis=1)
    back = exchange(tie(turned, *[plane.pieces[0] for plane in grad_planes])).astype(f32)
    qkv_sum = jnp.zeros((shard_rows, 3, model_width), f32)
    for r in range(PLANE):
        columns = back[r, :shard_rows].reshape(shard_rows, 3, PAIR)
        qkv_sum = lax.dynamic_update_slice(qkv_sum, columns, (0, 0, column(r)))
    small_sum = jnp.sum(back[:, shard_rows:], axis=0)
    qkv_sum = qkv_sum.reshape(shard_rows, 3 * model_width)
    small_sum = small_sum.reshape(-1)
    sums = []
    offset = 0
    for item in small:
        sums.append(small_sum[offset : offset + item.shape[0]])
        offset += item.shape[0]

    return (
        result_low.reshape(micro_count, tok_dev, model_width),
        stream_low.reshape(micro_count, tok_dev, model_width),
        sums[0],
        sums[1],
        qkv_sum,
        sums[2],
        sums[3],
        out_sum,
        sums[4],
        sums[5],
        sums[6],
        up_sum,
        sums[8],
        down_sum,
        sums[7],
    )


def solution(mesh):
    return jax.shard_map(
        body,
        mesh=mesh,
        in_specs=(
            P(None, "seq", None),
            P("seq"),
            P("seq"),
            P("seq", None),
            P("seq"),
            P("seq"),
            P("seq", None),
            P("seq"),
            P("seq"),
            P("seq"),
            P("seq", None),
            P("seq"),
            P("seq", None),
            P("seq"),
            P(None, "seq"),
            P(),
            P(None, "seq", None),
        ),
        out_specs=(
            P(None, "seq", None),
            P(None, "seq", None),
            P("seq"),
            P("seq"),
            P("seq", None),
            P("seq"),
            P("seq"),
            P("seq", None),
            P("seq"),
            P("seq"),
            P("seq"),
            P("seq", None),
            P("seq"),
            P("seq", None),
            P("seq"),
        ),
        check_vma=False,
    )
```

profile of v0, /device:TPU:0, one launch (start us, length us, event | category | flops | bytes accessed | tf_op | source)
XLA Modules:
  0.0 562.2 jit_solution(9608600360548576333)
XLA Ops:
  23.6 8.8 %collective-permute-done.4 = bf16[2,2,48,384]{3,2,1,0:T(8,128)(2,1)S(1)} collective-permute-done((bf16[2,2,48,384]{3,2,1,0:T(8,128)(2,1)S(1)}, bf16[2,2,48,384]{3,2,1,0:T(8,128)(2,1)S(1)}, u32[]{:S(2)}, u32[]{:S(2)}) %collective-permute-start.4) | collective-permute-done | bytes 147488 | tf_op jit(solution)/shard_map/ppermute | solution.py:39
  39.9 7.7 %collective-permute-done.5 = bf16[1,8,48,384]{3,2,1,0:T(8,128)(2,1)S(1)} collective-permute-done((bf16[1,8,48,384]{3,2,1,0:T(8,128)(2,1)S(1)}, bf16[1,8,48,384]{3,2,1,0:T(8,128)(2,1)S(1)}, u32[]{:S(2)}, u32[]{:S(2)}) %collective-permute-start.5) | collective-permute-done | bytes 294944 | tf_op jit(solution)/shard_map/ppermute | solution.py:39
  52.1 11.3 %collective-permute-done.6 = bf16[2,8,48,384]{3,2,1,0:T(8,128)(2,1)} collective-permute-done((bf16[2,8,48,384]{3,2,1,0:T(8,128)(2,1)}, bf16[2,8,48,384]{3,2,1,0:T(8,128)(2,1)}, u32[]{:S(2)}, u32[]{:S(2)}) %collective-permute-start.6) | collective-permute-done | bytes 589856 | tf_op jit(solution)/shard_map/ppermute | solution.py:39
  92.9 4.8 add_convert_fusion.1
  100.6 3.6 collective-permute-start.11
  106.4 24.1 %collective-permute-done.11.before = bf16[2,576,256]{2,1,0:T(8,128)(2,1)S(1)} collective-permute-done((bf16[2,576,256]{2,1,0:T(8,128)(2,1)}, bf16[2,576,256]{2,1,0:T(8,128)(2,1)S(1)}, u32[]{:S(2)}, u32[]{:S(2)}) %collective-permute-start.11) | collective-permute-done | bytes 589856 | tf_op jit(solution)/shard_map/ppermute | solution.py:45
  130.6 7.0 %collective-permute-done.12.after = bf16[2,576,256]{2,1,0:T(8,128)(2,1)S(1)} collective-permute-done((bf16[2,576,256]{2,1,0:T(8,128)(2,1)S(1)}, bf16[2,576,256]{2,1,0:T(8,128)(2,1)S(1)}, u32[]{:S(2)}, u32[]{:S(2)}) %collective-permute-start.12) | collective-permute-done | bytes 589856 | tf_op jit(solution)/shard_map/ppermute | solution.py:45
  138.4 33.3 %shard_map.272 = (bf16[8,2,256,128]{3,2,1,0:T(8,128)(2,1)}, f32[32,256]{1,0:T(8,128)}) custom-call(s32[3]{0:T(128)} %pad_add_fusion.info, s32[2,16]{1,0:T(2,128)} %concatenate.129.bounds, bf16[2,8,256,384]{3,2,1,0:T(8,128)(2,1)} %bitcast.592, bf16[2,576,256]{2,1,0:T(8,128)(2,1)} %copy-done.27, bf16[2,576,256]{2,1,0:T(8,128)(2,1)} %copy-done.28), custom_call_target="tpu_custom_call" | custom-call | flops 2684354560 | bytes 157286400 | tf_op jit(solution)/shard_map/pallas_call | solution.py:387
  182.8 5.0 collective-permute-done.14
  195.8 7.7 %all-gather.3.cloned.1.call-done = bf16[9216,1024]{1,0:T(8,128)(2,1)} async-done(((bf16[288,1024]{1,0:T(8,128)(2,1)}), bf16[9216,1024]{1,0:T(8,128)(2,1)}) %all-gather.3.cloned.1.call-update) | async-done | bytes 18874384 | tf_op jit(solution)/shard_map/all_gather | solution.py:588
  203.5 3.9 fusion.112
  207.4 4.7 fusion.113
  229.5 10.0 %fusion.137 = f32[512,1024]{1,0:T(8,128)S(1)} fusion(bf16[512,1024]{1,0:T(8,128)(2,1)S(1)} %get-tuple-element.292, bf16[1024,1024]{1,0:T(8,128)(2,1)S(1)} %bitcast.651), kind=kOutput, calls=%fused_computation.425 | convolution fusion | flops 1073741824 | bytes 5242880 | tf_op jit(solution)/shard_map/dot_general | solution.py:34
  253.2 4.4 fusion.111
  280.6 4.2 fusion.110
  313.9 18.8 %shard_map.273 = (f32[2048,128]{1,0:T(8,128)}, f32[2048,256]{1,0:T(8,128)}, bf16[768,256]{1,0:T(8,128)(2,1)}, bf16[768,256]{1,0:T(8,128)(2,1)}) custom-call(s32[3]{0:T(128)} %pad_add_fusion.info, s32[2,16]{1,0:T(2,128)} %concatenate.129.bounds, bf16[2,8,256,384]{3,2,1,0:T(8,128)(2,1)} %bitcast.593, bf16[2,576,256]{2,1,0:T(8,128)(2,1)} %copy-done.27, ...), custom_call_target="tpu_custom_call" | custom-call | flops 1342177280 | bytes 91750400 | tf_op jit(solution)/shard_map/pallas_call | solution.py:418
  334.2 6.0 %collective-permute-start.35 = (bf16[768,256]{1,0:T(8,128)(2,1)}, bf16[768,256]{1,0:T(8,128)(2,1)S(1)}, u32[]{:S(2)}, u32[]{:S(2)}) collective-permute-start(bf16[768,256]{1,0:T(8,128)(2,1)} %get-tuple-element.80), channel_id=1, source_target_pairs={{0,8},{1,9},{2,10},{3,11},{4,12},{5,13},{6,14},{7,15},{8,16},{9,17... | collective-permute-start | bytes 1179656 | tf_op jit(solution)/shard_map/ppermute | solution.py:45
  345.2 7.3 %collective-permute-done.33 = bf16[2,2,2,64,1024]{4,3,0,1,2:T(8,128)(2,1)} collective-permute-done((bf16[2,2,2,64,1024]{4,3,0,1,2:T(8,128)(2,1)}, bf16[2,2,2,64,1024]{4,3,0,1,2:T(8,128)(2,1)}, u32[]{:S(2)}, u32[]{:S(2)}) %collective-permute-start.33) | collective-permute-done | bytes 1048608 | tf_op jit(solution)/shard_map/ppermute | solution.py:39
  361.2 4.3 shard_map.274
  365.4 3.8 convolution_convert_fusion.1
  373.8 7.3 %fusion.3 = bf16[4096,1024]{1,0:T(8,128)(2,1)S(1)} fusion(f32[1024]{0:T(1024)S(1)} %copy-done.59, f32[1024]{0:T(1024)S(1)} %copy-done.53, f32[4096]{0:T(1024)S(1)} %bitcast.719, f32[4096]{0:T(1024)S(1)} %bitcast.718, bf16[1,8,256,1024]{3,2,1,0:T(8,128)(2,1)} %copy-done, bf16[1,8,256,1024]{3,2,1,0:T(8,128)(2,1)} %copy-done.1), kind=kLoop, calls=%fused_computation.5 | loop fusion | flops 29360128 | bytes 16818176 | tf_op jit(solution)/shard_map/convert_element_type | solution.py:607
  387.0 3.5 fusion.6
  399.4 19.0 %shard_map.275 = (f32[2048,128]{1,0:T(8,128)}, f32[2048,256]{1,0:T(8,128)}, bf16[768,256]{1,0:T(8,128)(2,1)}, bf16[768,256]{1,0:T(8,128)(2,1)}) custom-call(s32[3]{0:T(128)} %pad_add_fusion.info, s32[2,16]{1,0:T(2,128)} %concatenate.129.bounds, bf16[2,8,256,384]{3,2,1,0:T(8,128)(2,1)} %bitcast.594, bf16[2,576,256]{2,1,0:T(8,128)(2,1)} %copy-done.27, ...), custom_call_target="tpu_custom_call" | custom-call | flops 1342177280 | bytes 91750400 | tf_op jit(solution)/shard_map/pallas_call | solution.py:418
  419.9 5.5 collective-permute-start.44
  436.6 4.1 shard_map.276
  440.7 3.8 convolution_convert_fusion
  455.1 5.6 %fusion.25 = f32[1024,384]{1,0:T(8,128)S(1)} fusion(f32[1024,384]{1,0:T(8,128)} %fusion.6, bf16[2048,384]{1,0:T(8,128)(2,1)} %bitcast.609, bf16[4096,1024]{1,0:T(8,128)(2,1)} %copy-done.8), kind=kOutput, calls=%fused_computation.97 | convolution fusion | flops 1611005952 | bytes 8912896 | tf_op jit(solution)/shard_map/dot_general | solution.py:30
  465.0 5.8 %collective-permute-done.39 = bf16[1,256,1024]{2,1,0:T(8,128)(2,1)S(1)} collective-permute-done((bf16[1,256,1024]{2,1,0:T(8,128)(2,1)}, bf16[1,256,1024]{2,1,0:T(8,128)(2,1)S(1)}, u32[]{:S(2)}, u32[]{:S(2)}) %collective-permute-start.39) | collective-permute-done | bytes 524320 | tf_op jit(solution)/shard_map/ppermute | solution.py:39
  481.1 14.8 %collective-permute-done.47 = bf16[2,256,1024]{2,1,0:T(8,128)(2,1)} collective-permute-done((bf16[2,256,1024]{2,1,0:T(8,128)(2,1)}, bf16[2,256,1024]{2,1,0:T(8,128)(2,1)}, u32[]{:S(2)}, u32[]{:S(2)}) %collective-permute-start.47) | collective-permute-done | bytes 1048608 | tf_op jit(solution)/shard_map/ppermute | solution.py:39
  506.7 6.8 %collective-permute-done.49 = bf16[2,8,40,384]{3,2,1,0:T(8,128)(2,1)S(1)} collective-permute-done((bf16[2,8,40,384]{3,2,1,0:T(8,128)(2,1)S(1)}, bf16[2,8,40,384]{3,2,1,0:T(8,128)(2,1)S(1)}, u32[]{:S(2)}, u32[]{:S(2)}) %collective-permute-start.49) | collective-permute-done | bytes 491552 | tf_op jit(solution)/shard_map/ppermute | solution.py:39
  517.7 9.8 %collective-permute-done.60 = bf16[64,1024]{1,0:T(8,128)(2,1)S(1)} collective-permute-done((bf16[64,1024]{1,0:T(8,128)(2,1)S(1)}, bf16[64,1024]{1,0:T(8,128)(2,1)S(1)}, u32[]{:S(2)}, u32[]{:S(2)}) %collective-permute-start.60) | collective-permute-done | bytes 131104 | tf_op jit(solution)/shard_map/ppermute | solution.py:39
  542.8 4.3 collective-permute-done.56
  (524 shorter events, 274.6 us)
Async XLA Ops:
  7.2 196.3 %all-gather.3.cloned.1.call-start = ((), (), s32[]{:S(2)}) async-start(), calls=%async_computation | async-start | bytes 19464192 | tf_op jit(solution)/shard_map/all_gather | solution.py:588
  15.5 20.2 %collective-permute-start.8 = (bf16[1,256,1024]{2,1,0:T(8,128)(2,1)S(1)}, bf16[1,256,1024]{2,1,0:T(8,128)(2,1)S(1)}, u32[]{:S(2)}, u32[]{:S(2)}) collective-permute-start(bf16[1,256,1024]{2,1,0:T(8,128)(2,1)S(1)} %get-tuple-element.231), channel_id=1, source_target_pairs={{0,4},{1,5},{2,6},{3,7},{4,0},{5,1},{6,2},{7,3},{8,12},{9,13},{10,... | collective-permute-start | bytes 1572872 | tf_op jit(solution)/shard_map/ppermute | solution.py:39
  36.8 29.0 %collective-permute-start.9 = (bf16[2,256,1024]{2,1,0:T(8,128)(2,1)}, bf16[2,256,1024]{2,1,0:T(8,128)(2,1)}, u32[]{:S(2)}, u32[]{:S(2)}) collective-permute-start(bf16[2,256,1024]{2,1,0:T(8,128)(2,1)} %pad_maximum_fusion.16), channel_id=1, source_target_pairs={{0,2},{1,3},{2,0},{3,1},{4,6},{5,7},{6,4},{7,5},{8,10},{9,11},{10,... | collective-permute-start | bytes 3145736 | tf_op jit(solution)/shard_map/ppermute | solution.py:39
  38.4 27.4 %collective-permute-start.1 = (bf16[2,256,1024]{2,1,0:T(8,128)(2,1)}, bf16[2,256,1024]{2,1,0:T(8,128)(2,1)S(1)}, u32[]{:S(2)}, u32[]{:S(2)}) collective-permute-start(bf16[2,256,1024]{2,1,0:T(8,128)(2,1)} %pad_maximum_fusion.15), channel_id=1, source_target_pairs={{0,4},{1,5},{2,6},{3,7},{4,0},{5,1},{6,2},{7,3},{8,12},{9,13},{10,... | collective-permute-start | bytes 3145736 | tf_op jit(solution)/shard_map/ppermute | solution.py:39
  100.6 29.9 %collective-permute-start.11 = (bf16[2,576,256]{2,1,0:T(8,128)(2,1)}, bf16[2,576,256]{2,1,0:T(8,128)(2,1)S(1)}, u32[]{:S(2)}, u32[]{:S(2)}) collective-permute-start(bf16[2,576,256]{2,1,0:T(8,128)(2,1)} %fusion.59), channel_id=1, source_target_pairs={{0,8},{1,9},{2,10},{3,11},{4,12},{5,13},{6,14},{7,15},{8,16},{9,17... | collective-permute-start | bytes 1769480 | tf_op jit(solution)/shard_map/ppermute | solution.py:45
  104.3 33.3 %collective-permute-start.12 = (bf16[2,576,256]{2,1,0:T(8,128)(2,1)S(1)}, bf16[2,576,256]{2,1,0:T(8,128)(2,1)S(1)}, u32[]{:S(2)}, u32[]{:S(2)}) collective-permute-start(bf16[2,576,256]{2,1,0:T(8,128)(2,1)S(1)} %fusion.57), channel_id=1, source_target_pairs={{8,0},{9,1},{10,2},{11,3},{12,4},{13,5},{14,6},{15,7},{16,8},{17,9... | collective-permute-start | bytes 1769480 | tf_op jit(solution)/shard_map/ppermute | solution.py:45
  174.4 20.7 %collective-permute-start.19 = (bf16[2,256,128]{2,1,0:T(8,128)(2,1)S(1)}, bf16[2,256,128]{2,1,0:T(8,128)(2,1)S(1)}, u32[]{:S(2)}, u32[]{:S(2)}) collective-permute-start(bf16[2,256,128]{2,1,0:T(8,128)(2,1)S(1)} %get-tuple-element.223), channel_id=1, source_target_pairs={{0,7},{1,6},{2,5},{3,4},{4,3},{5,2},{6,1},{7,0},{8,15},{9,14},{10,... | collective-permute-start | bytes 393224 | tf_op jit(solution)/shard_map/ppermute | solution.py:39
  280.0 26.4 %collective-permute-start.22 = (bf16[2,2,2,2,80,1024]{5,4,3,2,1,0:T(8,128)(2,1)S(1)}, bf16[2,2,2,2,80,1024]{5,4,3,2,1,0:T(8,128)(2,1)S(1)}, u32[]{:S(2)}, u32[]{:S(2)}) collective-permute-start(bf16[2,2,2,2,80,1024]{5,4,3,2,1,0:T(8,128)(2,1)S(1)} %pad_maximum_fusion.1), channel_id=1, source_target_pairs={{0,1},{1,0},{2,3},{3,2},{4,5},{5,4},{6,7},{7,6},{8,9},{9,8},{10,11... | collective-permute-start | bytes 7864328 | tf_op jit(solution)/shard_map/ppermute | solution.py:39
  280.3 26.1 %collective-permute-start.30 = (bf16[2,2,2,2,80,1024]{5,4,0,1,3,2:T(8,128)(2,1)S(1)}, bf16[2,2,2,2,80,1024]{5,4,0,1,3,2:T(8,128)(2,1)S(1)}, u32[]{:S(2)}, u32[]{:S(2)}) collective-permute-start(bf16[2,2,2,2,80,1024]{5,4,0,1,3,2:T(8,128)(2,1)S(1)} %copy.185), channel_id=1, source_target_pairs={{0,1},{1,0},{2,3},{3,2},{4,5},{5,4},{6,7},{7,6},{8,9},{9,8},{10,11... | collective-permute-start | bytes 7864328 | tf_op jit(solution)/shard_map/ppermute | solution.py:39
  303.7 30.5 %collective-permute-start.34 = (bf16[2,2,2,64,1024]{4,3,0,2,1:T(8,128)(2,1)}, bf16[2,2,2,64,1024]{4,3,0,2,1:T(8,128)(2,1)}, u32[]{:S(2)}, u32[]{:S(2)}) collective-permute-start(bf16[2,2,2,64,1024]{4,3,0,2,1:T(8,128)(2,1)} %get-tuple-element.152), channel_id=1, source_target_pairs={{0,8},{1,9},{2,10},{3,11},{4,12},{5,13},{6,14},{7,15},{8,0},{9,1},... | collective-permute-start | bytes 3145736 | tf_op jit(solution)/shard_map/ppermute | solution.py:39
  309.0 45.5 %collective-permute-start.32 = (bf16[2,2,2,80,1024]{4,3,0,2,1:T(8,128)(2,1)}, bf16[2,2,2,80,1024]{4,3,0,2,1:T(8,128)(2,1)}, u32[]{:S(2)}, u32[]{:S(2)}) collective-permute-start(bf16[2,2,2,80,1024]{4,3,0,2,1:T(8,128)(2,1)} %copy.166), channel_id=1, source_target_pairs={{0,4},{1,5},{2,6},{3,7},{4,0},{5,1},{6,2},{7,3},{8,12},{9,13},{10,... | collective-permute-start | bytes 3932168 | tf_op jit(solution)/shard_map/ppermute | solution.py:39
  311.8 42.7 %collective-permute-start.31 = (bf16[2,2,2,80,1024]{4,3,0,1,2:T(8,128)(2,1)}, bf16[2,2,2,80,1024]{4,3,0,1,2:T(8,128)(2,1)}, u32[]{:S(2)}, u32[]{:S(2)}) collective-permute-start(bf16[2,2,2,80,1024]{4,3,0,1,2:T(8,128)(2,1)} %fusion.28), channel_id=1, source_target_pairs={{0,2},{1,3},{2,0},{3,1},{4,6},{5,7},{6,4},{7,5},{8,10},{9,11},{10,... | collective-permute-start | bytes 3932168 | tf_op jit(solution)/shard_map/ppermute | solution.py:39
  312.5 40.0 %collective-permute-start.33 = (bf16[2,2,2,64,1024]{4,3,0,1,2:T(8,128)(2,1)}, bf16[2,2,2,64,1024]{4,3,0,1,2:T(8,128)(2,1)}, u32[]{:S(2)}, u32[]{:S(2)}) collective-permute-start(bf16[2,2,2,64,1024]{4,3,0,1,2:T(8,128)(2,1)} %fusion.34), channel_id=1, source_target_pairs={{0,8},{1,9},{2,10},{3,11},{4,12},{5,13},{6,14},{7,15},{8,0},{9,1},... | collective-permute-start | bytes 3145736 | tf_op jit(solution)/shard_map/ppermute | solution.py:39
  332.8 27.1 %collective-permute-start.36 = (bf16[768,256]{1,0:T(8,128)(2,1)}, bf16[768,256]{1,0:T(8,128)(2,1)S(1)}, u32[]{:S(2)}, u32[]{:S(2)}) collective-permute-start(bf16[768,256]{1,0:T(8,128)(2,1)} %get-tuple-element.73), channel_id=1, source_target_pairs={{8,0},{9,1},{10,2},{11,3},{12,4},{13,5},{14,6},{15,7},{16,8},{17,9... | collective-permute-start | bytes 1179656 | tf_op jit(solution)/shard_map/ppermute | solution.py:45
  334.2 25.4 %collective-permute-start.35 = (bf16[768,256]{1,0:T(8,128)(2,1)}, bf16[768,256]{1,0:T(8,128)(2,1)S(1)}, u32[]{:S(2)}, u32[]{:S(2)}) collective-permute-start(bf16[768,256]{1,0:T(8,128)(2,1)} %get-tuple-element.80), channel_id=1, source_target_pairs={{0,8},{1,9},{2,10},{3,11},{4,12},{5,13},{6,14},{7,15},{8,16},{9,17... | collective-permute-start | bytes 1179656 | tf_op jit(solution)/shard_map/ppermute | solution.py:45
  372.9 17.7 %collective-permute-start.37 = (bf16[4,256,1024]{2,1,0:T(8,128)(2,1)}, bf16[4,256,1024]{2,1,0:T(8,128)(2,1)}, u32[]{:S(2)}, u32[]{:S(2)}) collective-permute-start(bf16[4,256,1024]{2,1,0:T(8,128)(2,1)} %pad_maximum_fusion.11), channel_id=1, source_target_pairs={{0,1},{1,0},{2,3},{3,2},{4,5},{5,4},{6,7},{7,6},{8,9},{9,8},{10,11... | collective-permute-start | bytes 6291464 | tf_op jit(solution)/shard_map/ppermute | solution.py:39
  382.0 37.8 %collective-permute-start.42 = (bf16[2,2,64,1024]{3,2,0,1:T(8,128)(2,1)}, bf16[2,2,64,1024]{3,2,0,1:T(8,128)(2,1)}, u32[]{:S(2)}, u32[]{:S(2)}) collective-permute-start(bf16[2,2,64,1024]{3,2,0,1:T(8,128)(2,1)} %fusion.61), channel_id=1, source_target_pairs={{0,2},{1,3},{2,0},{3,1},{4,6},{5,7},{6,4},{7,5},{8,10},{9,11},{10,... | collective-permute-start | bytes 1572872 | tf_op jit(solution)/shard_map/ppermute | solution.py:39
  383.4 34.9 %collective-permute-start.43 = (bf16[2,2,64,1024]{3,2,1,0:T(8,128)(2,1)}, bf16[2,2,64,1024]{3,2,1,0:T(8,128)(2,1)}, u32[]{:S(2)}, u32[]{:S(2)}) collective-permute-start(bf16[2,2,64,1024]{3,2,1,0:T(8,128)(2,1)} %copy.175), channel_id=1, source_target_pairs={{0,4},{1,5},{2,6},{3,7},{4,0},{5,1},{6,2},{7,3},{8,12},{9,13},{10,... | collective-permute-start | bytes 1572872 | tf_op jit(solution)/shard_map/ppermute | solution.py:39
  385.0 34.9 %collective-permute-start.40 = (bf16[2,2,80,1024]{3,2,0,1:T(8,128)(2,1)}, bf16[2,2,80,1024]{3,2,0,1:T(8,128)(2,1)}, u32[]{:S(2)}, u32[]{:S(2)}) collective-permute-start(bf16[2,2,80,1024]{3,2,0,1:T(8,128)(2,1)} %fusion.51), channel_id=1, source_target_pairs={{0,4},{1,5},{2,6},{3,7},{4,0},{5,1},{6,2},{7,3},{8,12},{9,13},{10,... | collective-permute-start | bytes 1966088 | tf_op jit(solution)/shard_map/ppermute | solution.py:39
  386.4 33.4 %collective-permute-start.41 = (bf16[2,2,80,1024]{3,2,1,0:T(8,128)(2,1)}, bf16[2,2,80,1024]{3,2,1,0:T(8,128)(2,1)}, u32[]{:S(2)}, u32[]{:S(2)}) collective-permute-start(bf16[2,2,80,1024]{3,2,1,0:T(8,128)(2,1)} %copy.172), channel_id=1, source_target_pairs={{0,2},{1,3},{2,0},{3,1},{4,6},{5,7},{6,4},{7,5},{8,10},{9,11},{10,... | collective-permute-start | bytes 1966088 | tf_op jit(solution)/shard_map/ppermute | solution.py:39
  393.6 40.5 %collective-permute-start.38 = (bf16[2,256,1024]{2,1,0:T(8,128)(2,1)}, bf16[2,256,1024]{2,1,0:T(8,128)(2,1)}, u32[]{:S(2)}, u32[]{:S(2)}) collective-permute-start(bf16[2,256,1024]{2,1,0:T(8,128)(2,1)} %pad_maximum_fusion.17), channel_id=1, source_target_pairs={{0,2},{1,3},{2,0},{3,1},{4,6},{5,7},{6,4},{7,5},{8,10},{9,11},{10,... | collective-permute-start | bytes 3145736 | tf_op jit(solution)/shard_map/ppermute | solution.py:39
  418.4 18.2 %collective-permute-start.45 = (bf16[768,256]{1,0:T(8,128)(2,1)}, bf16[768,256]{1,0:T(8,128)(2,1)}, u32[]{:S(2)}, u32[]{:S(2)}) collective-permute-start(bf16[768,256]{1,0:T(8,128)(2,1)} %get-tuple-element.84), channel_id=1, source_target_pairs={{8,0},{9,1},{10,2},{11,3},{12,4},{13,5},{14,6},{15,7},{16,8},{17,9... | collective-permute-start | bytes 1179656 | tf_op jit(solution)/shard_map/ppermute | solution.py:45
  450.6 48.8 %collective-permute-start.52 = (bf16[2,64,1024]{2,1,0:T(8,128)(2,1)}, bf16[2,64,1024]{2,1,0:T(8,128)(2,1)}, u32[]{:S(2)}, u32[]{:S(2)}) collective-permute-start(bf16[2,64,1024]{2,1,0:T(8,128)(2,1)} %get-tuple-element.194), channel_id=1, source_target_pairs={{0,4},{1,5},{2,6},{3,7},{4,0},{5,1},{6,2},{7,3},{8,12},{9,13},{10,... | collective-permute-start | bytes 786440 | tf_op jit(solution)/shard_map/ppermute | solution.py:39
  451.3 47.2 %collective-permute-start.53 = (bf16[2,64,1024]{2,1,0:T(8,128)(2,1)}, bf16[2,64,1024]{2,1,0:T(8,128)(2,1)}, u32[]{:S(2)}, u32[]{:S(2)}) collective-permute-start(bf16[2,64,1024]{2,1,0:T(8,128)(2,1)} %get-tuple-element.192), channel_id=1, source_target_pairs={{0,2},{1,3},{2,0},{3,1},{4,6},{5,7},{6,4},{7,5},{8,10},{9,11},{10,... | collective-permute-start | bytes 786440 | tf_op jit(solution)/shard_map/ppermute | solution.py:39
  452.7 46.7 %collective-permute-start.50 = (bf16[2,80,1024]{2,1,0:T(8,128)(2,1)}, bf16[2,80,1024]{2,1,0:T(8,128)(2,1)}, u32[]{:S(2)}, u32[]{:S(2)}) collective-permute-start(bf16[2,80,1024]{2,1,0:T(8,128)(2,1)} %get-tuple-element.190), channel_id=1, source_target_pairs={{0,8},{1,9},{2,10},{3,11},{4,12},{5,13},{6,14},{7,15},{8,0},{9,1},... | collective-permute-start | bytes 983048 | tf_op jit(solution)/shard_map/ppermute | solution.py:39
  461.0 38.4 %collective-permute-start.51 = (bf16[2,80,1024]{2,1,0:T(8,128)(2,1)}, bf16[2,80,1024]{2,1,0:T(8,128)(2,1)}, u32[]{:S(2)}, u32[]{:S(2)}) collective-permute-start(bf16[2,80,1024]{2,1,0:T(8,128)(2,1)} %get-tuple-element.188), channel_id=1, source_target_pairs={{0,8},{1,9},{2,10},{3,11},{4,12},{5,13},{6,14},{7,15},{8,0},{9,1},... | collective-permute-start | bytes 983048 | tf_op jit(solution)/shard_map/ppermute | solution.py:39
  470.8 25.1 %collective-permute-start.47 = (bf16[2,256,1024]{2,1,0:T(8,128)(2,1)}, bf16[2,256,1024]{2,1,0:T(8,128)(2,1)}, u32[]{:S(2)}, u32[]{:S(2)}) collective-permute-start(bf16[2,256,1024]{2,1,0:T(8,128)(2,1)} %pad_maximum_fusion.18), channel_id=1, source_target_pairs={{0,4},{1,5},{2,6},{3,7},{4,0},{5,1},{6,2},{7,3},{8,12},{9,13},{10,... | collective-permute-start | bytes 3145736 | tf_op jit(solution)/shard_map/ppermute | solution.py:39
  498.4 39.7 %collective-permute-start.48 = (bf16[1,256,1024]{2,1,0:T(8,128)(2,1)S(1)}, bf16[1,256,1024]{2,1,0:T(8,128)(2,1)S(1)}, u32[]{:S(2)}, u32[]{:S(2)}) collective-permute-start(bf16[1,256,1024]{2,1,0:T(8,128)(2,1)S(1)} %add_convert_fusion.11), channel_id=1, source_target_pairs={{0,2},{1,3},{2,0},{3,1},{4,6},{5,7},{6,4},{7,5},{8,10},{9,11},{10,... | collective-permute-start | bytes 1572872 | tf_op jit(solution)/shard_map/ppermute | solution.py:39
  501.8 25.7 %collective-permute-start.60 = (bf16[64,1024]{1,0:T(8,128)(2,1)S(1)}, bf16[64,1024]{1,0:T(8,128)(2,1)S(1)}, u32[]{:S(2)}, u32[]{:S(2)}) collective-permute-start(bf16[64,1024]{1,0:T(8,128)(2,1)S(1)} %fusion.94), channel_id=1, source_target_pairs={{0,16},{1,17},{2,18},{3,19},{4,20},{5,21},{6,22},{7,23},{8,24},{9,... | collective-permute-start | bytes 393224 | tf_op jit(solution)/shard_map/ppermute | solution.py:39
  505.3 25.7 %collective-permute-start.59 = (bf16[80,1024]{1,0:T(8,128)(2,1)S(1)}, bf16[80,1024]{1,0:T(8,128)(2,1)S(1)}, u32[]{:S(2)}, u32[]{:S(2)}) collective-permute-start(bf16[80,1024]{1,0:T(8,128)(2,1)S(1)} %fusion.85), channel_id=1, source_target_pairs={{0,16},{1,17},{2,18},{3,19},{4,20},{5,21},{6,22},{7,23},{8,24},{9,... | collective-permute-start | bytes 491528 | tf_op jit(solution)/shard_map/ppermute | solution.py:39
  513.6 21.0 %collective-permute-start.58 = (bf16[80,1024]{1,0:T(8,128)(2,1)S(1)}, bf16[80,1024]{1,0:T(8,128)(2,1)S(1)}, u32[]{:S(2)}, u32[]{:S(2)}) collective-permute-start(bf16[80,1024]{1,0:T(8,128)(2,1)S(1)} %fusion.84), channel_id=1, source_target_pairs={{0,16},{1,17},{2,18},{3,19},{4,20},{5,21},{6,22},{7,23},{8,24},{9,... | collective-permute-start | bytes 491528 | tf_op jit(solution)/shard_map/ppermute | solution.py:39
  513.7 24.3 %collective-permute-start.54 = (bf16[1,8,40,384]{3,2,1,0:T(8,128)(2,1)S(1)}, bf16[1,8,40,384]{3,2,1,0:T(8,128)(2,1)S(1)}, u32[]{:S(2)}, u32[]{:S(2)}) collective-permute-start(bf16[1,8,40,384]{3,2,1,0:T(8,128)(2,1)S(1)} %slice_bitcast_fusion.17), channel_id=1, source_target_pairs={{0,16},{1,17},{2,18},{3,19},{4,20},{5,21},{6,22},{7,23},{8,24},{9,... | collective-permute-start | bytes 737288 | tf_op jit(solution)/shard_map/ppermute | solution.py:39
  (109 other events, 825.0 us)
Sparse Core Ops, SparseCore 0:
  66.0 137.4 all-gather.2
where the time goes:
time: 573 us; the launch traced here: 562 us
  waiting for transfers between devices  141 us (25%)
  other arithmetic  108 us (19%)
  Pallas kernels  85.5 us (15%)
  matrix products  82.5 us (14%)
  starting transfers between devices  72.4 us (13%)
  local copies, waits for them, and re-layouts  55.6 us (10%)
  between operations  16.4 us (3%)
    ppermute x56, waiting for transfers between devices, swap(): return lax.ppermute(block, 'seq', [(i, i ^ bit) for i in range(n)])  102 us
    ppermute x56, starting transfers between devices, swap(): return lax.ppermute(block, 'seq', [(i, i ^ bit) for i in range(n)])  52.8 us
    pallas_call x2, Pallas kernels, attend_back(): pl.pallas_call(functools.partial(attend_back_kernel, m, orders), grid_spe...  37.8 us
    convert_element_type x20, other arithmetic, half(): return (kept + pick(self.got, axis, index).astype(f32)).astype(bf16)  37.1 us
    dot_general x11, matrix products, product_nt(): lax.dot_general(left, right, (((1,), (1,)), ((), ())), preferred_element_...  33.8 us
    pallas_call x1, Pallas kernels, attend(): pl.pallas_call(functools.partial(attend_kernel, orders), grid_spec=pltpu....  33.3 us
    ppermute x6, waiting for transfers between devices, shift_plane(): lax.ppermute(block, 'seq', [(i, i + step) for i in range(n) if 0 <= i + s...  31.4 us
    dot_general x10, matrix products, product(): return jnp.dot(left, right, preferred_element_type=f32)  26.5 us
  transfers between devices with their start and end apart: 63, of which 26 were waited for; matrix products, arithmetic and copies ran while one was open for 28% of the time, Pallas kernels for 14%

commit v1 on v0

--- a/solution.py
+++ b/solution.py
@@ -15,6 +15,7 @@
 LEAD = 640
 WINDOW = 640
 TILE = 256
+WIDE = 512
 
 epsilon = 1e-05
 negative_fill = -1e30
@@ -209,9 +210,9 @@
     for copy in started:
         copy.start()
     value_t[:, HEAD_DIM:, :] = jnp.ones((2, 16, WINDOW), bf16)
-    lanes = lax.broadcasted_iota(jnp.int32, (TILE, PAIR), 1)
-    rows_iota = lax.broadcasted_iota(jnp.int32, (TILE, PAIR), 0)
-    lane_row = lax.broadcasted_iota(jnp.int32, (1, TILE), 1)
+    lanes = lax.broadcasted_iota(jnp.int32, (WIDE, PAIR), 1)
+    rows_iota = lax.broadcasted_iota(jnp.int32, (WIDE, PAIR), 0)
+    lane_row = lax.broadcasted_iota(jnp.int32, (1, WIDE), 1)
     query_mark = jnp.where(lanes == 0, 1.0, 0.0).astype(bf16)
     for copy in started:
         copy.wait()
@@ -228,12 +229,12 @@
                 turned = values[m, pl.ds(key_start, WINDOW), :].astype(f32).T
                 value_t[0, :HEAD_DIM, :] = turned[:HEAD_DIM].astype(bf16)
                 value_t[1, :HEAD_DIM, :] = turned[HEAD_DIM:].astype(bf16)
-                first_tile = jnp.maximum(begin - LEAD, 0) >> 8
-                last_tile = (jnp.minimum(finish - LEAD, own) + TILE - 1) >> 8
+                first_tile = jnp.maximum(begin - LEAD, 0) >> (WIDE.bit_length() - 1)
+                last_tile = (jnp.minimum(finish - LEAD, own) + WIDE - 1) >> (WIDE.bit_length() - 1)
 
                 def one_tile(tile, carry):
-                    spot = pl.multiple_of(tile * TILE, TILE)
-                    scaled = queries[m, pl.ds(spot, TILE), :].astype(f32) * (HEAD_DIM**-0.5)
+                    spot = pl.multiple_of(tile * WIDE, WIDE)
+                    scaled = queries[m, pl.ds(spot, WIDE), :].astype(f32) * (HEAD_DIM**-0.5)
                     pieces = []
                     inside_lane = (lane_row + (spot + LEAD) >= begin) & (lane_row + (spot + LEAD) < finish)
                     for h, query in enumerate(split_heads(scaled, lanes)):
@@ -244,15 +245,15 @@
                         out = product(value_t[h], weights)
                         total = out[HEAD_DIM : HEAD_DIM + 1]
                         pieces.append(out[:HEAD_DIM] / total)
-                        row = (m * 2 + h) * blocks + tile
+                        row = (m * 2 + h) * (own // WIDE) + tile
                         stats[pl.ds(row, 1), :] = jnp.where(
                             inside_lane, peak + jnp.log(total), stats[pl.ds(row, 1), :]
                         )
                     value = jnp.concatenate(pieces, axis=0).T
                     place_row = rows_iota + (spot + LEAD)
                     inside = (place_row >= begin) & (place_row < finish)
-                    result[m, pl.ds(spot, TILE), :] = jnp.where(
-                        inside, value, result[m, pl.ds(spot, TILE), :]
+                    result[m, pl.ds(spot, WIDE), :] = jnp.where(
+                        inside, value, result[m, pl.ds(spot, WIDE), :]
                     )
                     return carry
 
@@ -383,14 +384,14 @@
     micro_count, blocks, rows, _ = qkv.shape
     own = blocks * rows
     span = LEAD + own + LEAD
-    stat_rows = micro_count * 2 * blocks
+    stat_rows = micro_count * 2 * (own // WIDE)
     return pl.pallas_call(
         functools.partial(attend_kernel, orders),
         grid_spec=pltpu.PrefetchScalarGridSpec(
             num_scalar_prefetch=2,
             grid=(1,),
             in_specs=any_specs(3),
-            out_specs=any_specs(1) + [pl.BlockSpec((stat_rows, TILE), lambda g, a, b: (0, 0))],
+            out_specs=any_specs(1) + [pl.BlockSpec((stat_rows, WIDE), lambda g, a, b: (0, 0))],
             scratch_shapes=[
                 pltpu.VMEM((micro_count, own, PAIR), bf16),
                 pltpu.VMEM((micro_count, span, PAIR), bf16),
@@ -404,7 +405,7 @@
         ),
         out_shape=[
             jax.ShapeDtypeStruct((blocks, micro_count, rows, PAIR), bf16),
-            jax.ShapeDtypeStruct((stat_rows, TILE), f32),
+            jax.ShapeDtypeStruct((stat_rows, WIDE), f32),
         ],
         cost_estimate=cover(micro_count * own, 30),
     )(info, bounds, qkv, before, after)
@@ -627,6 +628,7 @@
     before = shift_plane(last_rows[:, edge_blocks * tok_dev - HALO :], 1)
     after = shift_plane(first_rows[:, :HALO], -1)
     mixed_pair, stats = attend(token_orders, info, bounds, qkv, before, after)
+    stats = stats.reshape(-1, TILE)
 
     def column(r):
         return jnp.bitwise_xor(mine, r) * PAIR

time: 573 us -> 577 us (level)
  waiting for transfers between devices: 141 us -> 155 us
    all_gather x1, waiting for transfers between devices: 7.75 us -> 17.3 us  [body(): every = lax.all_gather(packed, 'seq')]
    unnamed x171 -> x185, local copies, waits for them, and re-layouts: 17.1 us -> 18.5 us
  transfers between devices with their start and end apart: 63 -> 63, of which waited for: 26 -> 26; matrix products, arithmetic and copies ran while one was open for 28% -> 27% of each run, Pallas kernels for 14% -> 13%
where the time goes in v1:
time: 577 us; the launch traced here: 568 us
  waiting for transfers between devices  155 us (27%)
  other arithmetic  111 us (19%)
  Pallas kernels  82.7 us (14%)
  matrix products  76.8 us (13%)
  starting transfers between devices  72.5 us (13%)
  local copies, waits for them, and re-layouts  53.2 us (9%)
  between operations  16.6 us (3%)
    ppermute x56, waiting for transfers between devices, swap(): return lax.ppermute(block, 'seq', [(i, i ^ bit) for i in range(n)])  106 us
    ppermute x56, starting transfers between devices, swap(): return lax.ppermute(block, 'seq', [(i, i ^ bit) for i in range(n)])  53.6 us
    convert_element_type x20, other arithmetic, half(): return (kept + pick(self.got, axis, index).astype(f32)).astype(bf16)  39.7 us
    pallas_call x2, Pallas kernels, attend_back(): pl.pallas_call(functools.partial(attend_back_kernel, m, orders), grid_spe...  39.3 us
    dot_general x11, matrix products, product_nt(): lax.dot_general(left, right, (((1,), (1,)), ((), ())), preferred_element_...  31.7 us
    ppermute x6, waiting for transfers between devices, shift_plane(): lax.ppermute(block, 'seq', [(i, i + step) for i in range(n) if 0 <= i + s...  31.2 us
    pallas_call x1, Pallas kernels, attend(): pl.pallas_call(functools.partial(attend_kernel, orders), grid_spec=pltpu....  29.1 us
    dot_general x10, matrix products, product(): return jnp.dot(left, right, preferred_element_type=f32)  24.1 us
  transfers between devices with their start and end apart: 63, of which 26 were waited for; matrix products, arithmetic and copies ran while one was open for 27% of the time, Pallas kernels for 13%

profile of v1, /device:TPU:0, one launch (start us, length us, event | category | flops | bytes accessed | tf_op | source)
XLA Modules:
  0.0 567.7 jit_solution(17613278421883535712)
XLA Ops:
  23.5 8.8 %collective-permute-done.4 = bf16[2,2,48,384]{3,2,1,0:T(8,128)(2,1)S(1)} collective-permute-done((bf16[2,2,48,384]{3,2,1,0:T(8,128)(2,1)S(1)}, bf16[2,2,48,384]{3,2,1,0:T(8,128)(2,1)S(1)}, u32[]{:S(2)}, u32[]{:S(2)}) %collective-permute-start.4) | collective-permute-done | bytes 147488 | tf_op jit(solution)/shard_map/ppermute | solution.py:40
  39.9 7.7 %collective-permute-done.5 = bf16[1,8,48,384]{3,2,1,0:T(8,128)(2,1)S(1)} collective-permute-done((bf16[1,8,48,384]{3,2,1,0:T(8,128)(2,1)S(1)}, bf16[1,8,48,384]{3,2,1,0:T(8,128)(2,1)S(1)}, u32[]{:S(2)}, u32[]{:S(2)}) %collective-permute-start.5) | collective-permute-done | bytes 294944 | tf_op jit(solution)/shard_map/ppermute | solution.py:40
  52.0 11.3 %collective-permute-done.6 = bf16[2,8,48,384]{3,2,1,0:T(8,128)(2,1)} collective-permute-done((bf16[2,8,48,384]{3,2,1,0:T(8,128)(2,1)}, bf16[2,8,48,384]{3,2,1,0:T(8,128)(2,1)}, u32[]{:S(2)}, u32[]{:S(2)}) %collective-permute-start.6) | collective-permute-done | bytes 589856 | tf_op jit(solution)/shard_map/ppermute | solution.py:40
  92.9 4.8 add_convert_fusion.1
  100.6 3.6 collective-permute-start.11
  106.4 24.1 %collective-permute-done.11.before = bf16[2,576,256]{2,1,0:T(8,128)(2,1)S(1)} collective-permute-done((bf16[2,576,256]{2,1,0:T(8,128)(2,1)}, bf16[2,576,256]{2,1,0:T(8,128)(2,1)S(1)}, u32[]{:S(2)}, u32[]{:S(2)}) %collective-permute-start.11) | collective-permute-done | bytes 589856 | tf_op jit(solution)/shard_map/ppermute | solution.py:46
  130.5 6.9 %collective-permute-done.12.after = bf16[2,576,256]{2,1,0:T(8,128)(2,1)S(1)} collective-permute-done((bf16[2,576,256]{2,1,0:T(8,128)(2,1)S(1)}, bf16[2,576,256]{2,1,0:T(8,128)(2,1)S(1)}, u32[]{:S(2)}, u32[]{:S(2)}) %collective-permute-start.12) | collective-permute-done | bytes 589856 | tf_op jit(solution)/shard_map/ppermute | solution.py:46
  138.3 29.1 %shard_map.272 = (bf16[8,2,256,128]{3,2,1,0:T(8,128)(2,1)}, f32[16,512]{1,0:T(8,128)}) custom-call(s32[3]{0:T(128)} %pad_add_fusion.info, s32[2,16]{1,0:T(2,128)} %concatenate.129.bounds, bf16[2,8,256,384]{3,2,1,0:T(8,128)(2,1)} %bitcast.592, bf16[2,576,256]{2,1,0:T(8,128)(2,1)} %copy-done.28, bf16[2,576,256]{2,1,0:T(8,128)(2,1)} %copy-done.29), custom_call_target="tpu_custom_call" | custom-call | flops 2684354560 | bytes 157286400 | tf_op jit(solution)/shard_map/pallas_call | solution.py:388
  176.3 11.4 %collective-permute-done.14 = bf16[2,256,128]{2,1,0:T(8,128)(2,1)S(1)} collective-permute-done((bf16[2,256,128]{2,1,0:T(8,128)(2,1)S(1)}, bf16[2,256,128]{2,1,0:T(8,128)(2,1)S(1)}, u32[]{:S(2)}, u32[]{:S(2)}) %collective-permute-start.14) | collective-permute-done | bytes 131104 | tf_op jit(solution)/shard_map/ppermute | solution.py:40
  193.3 17.3 %all-gather.3.cloned.1.call-done = bf16[9216,1024]{1,0:T(8,128)(2,1)} async-done(((bf16[288,1024]{1,0:T(8,128)(2,1)}), bf16[9216,1024]{1,0:T(8,128)(2,1)}) %all-gather.3.cloned.1.call-update) | async-done | bytes 18874384 | tf_op jit(solution)/shard_map/all_gather | solution.py:589
  210.6 3.9 fusion.112
  214.5 6.2 %fusion.113 = (bf16[32,32,1024]{2,1,0:T(8,128)(2,1)S(1)}, bf16[32,32,1024]{2,1,0:T(8,128)(2,1)S(1)}, bf16[32,32,1024]{2,1,0:T(8,128)(2,1)S(1)}, bf16[32,32,1024]{2,1,0:T(8,128)(2,1)S(1)}, bf16[32,32,1024]{2,1,0:T(8,128)(2,1)S(1)}) fusion(bf16[32,288,1024]{2,1,0:T(8,128)(2,1)} %bitcast.596), kind=kLoop, calls=%fused_computation.401 | loop fusion | bytes 20971520 | tf_op jit(solution)/shard_map/slice | solution.py:591
  234.4 10.6 %fusion.132 = (bf16[1024]{0:T(1024)(128)(2,1)S(1)}, bf16[512,1024]{1,0:T(8,128)(2,1)S(1)}) fusion(f32[512,1024]{1,0:T(8,128)S(1)} %fusion.133, f32[1024]{0:T(1024)S(1)} %add.748, bf16[1024,1024]{1,0:T(8,128)(2,1)S(1)} %bitcast.673, bf16[512,1024]{1,0:T(8,128)(2,1)S(1)} %bitcast.625), kind=kOutput, calls=%fused_computation.420 | convolution fusion | flops 1080032256 | bytes 6297600 | tf_op jit(solution)/shard_map/dot_general | solution.py:35
  258.4 4.3 fusion.111
  285.6 4.2 fusion.110
  322.4 18.9 %shard_map.273 = (f32[2048,128]{1,0:T(8,128)}, f32[2048,256]{1,0:T(8,128)}, bf16[768,256]{1,0:T(8,128)(2,1)}, bf16[768,256]{1,0:T(8,128)(2,1)}) custom-call(s32[3]{0:T(128)} %pad_add_fusion.info, s32[2,16]{1,0:T(2,128)} %concatenate.129.bounds, bf16[2,8,256,384]{3,2,1,0:T(8,128)(2,1)} %bitcast.593, bf16[2,576,256]{2,1,0:T(8,128)(2,1)} %copy-done.28, ...), custom_call_target="tpu_custom_call" | custom-call | flops 1342177280 | bytes 91750400 | tf_op jit(solution)/shard_map/pallas_call | solution.py:419
  342.7 5.3 collective-permute-start.35
  353.0 4.5 collective-permute-done.33
  365.7 4.2 shard_map.274
  369.9 3.8 convolution_convert_fusion.1
  378.2 7.3 %fusion.3 = bf16[4096,1024]{1,0:T(8,128)(2,1)S(1)} fusion(f32[1024]{0:T(1024)S(1)} %copy-done.66, f32[1024]{0:T(1024)S(1)} %copy-done.60, f32[4096]{0:T(1024)S(1)} %bitcast.719, f32[4096]{0:T(1024)S(1)} %bitcast.718, bf16[1,8,256,1024]{3,2,1,0:T(8,128)(2,1)} %copy-done, bf16[1,8,256,1024]{3,2,1,0:T(8,128)(2,1)} %copy-done.1), kind=kLoop, calls=%fused_computation.5 | loop fusion | flops 29360128 | bytes 16818176 | tf_op jit(solution)/shard_map/convert_element_type | solution.py:608
  391.4 3.5 fusion.6
  403.6 20.4 %shard_map.275 = (f32[2048,128]{1,0:T(8,128)}, f32[2048,256]{1,0:T(8,128)}, bf16[768,256]{1,0:T(8,128)(2,1)}, bf16[768,256]{1,0:T(8,128)(2,1)}) custom-call(s32[3]{0:T(128)} %pad_add_fusion.info, s32[2,16]{1,0:T(2,128)} %concatenate.129.bounds, bf16[2,8,256,384]{3,2,1,0:T(8,128)(2,1)} %bitcast.594, bf16[2,576,256]{2,1,0:T(8,128)(2,1)} %copy-done.28, ...), custom_call_target="tpu_custom_call" | custom-call | flops 1342177280 | bytes 91750400 | tf_op jit(solution)/shard_map/pallas_call | solution.py:419
  425.5 5.5 collective-permute-start.44
  442.3 4.1 shard_map.276
  446.4 3.8 convolution_convert_fusion
  459.7 5.6 fusion.25
  470.7 5.8 %collective-permute-done.39 = bf16[1,256,1024]{2,1,0:T(8,128)(2,1)S(1)} collective-permute-done((bf16[1,256,1024]{2,1,0:T(8,128)(2,1)}, bf16[1,256,1024]{2,1,0:T(8,128)(2,1)S(1)}, u32[]{:S(2)}, u32[]{:S(2)}) %collective-permute-start.39) | collective-permute-done | bytes 524320 | tf_op jit(solution)/shard_map/ppermute | solution.py:40
  486.8 14.7 %collective-permute-done.47 = bf16[2,256,1024]{2,1,0:T(8,128)(2,1)} collective-permute-done((bf16[2,256,1024]{2,1,0:T(8,128)(2,1)}, bf16[2,256,1024]{2,1,0:T(8,128)(2,1)}, u32[]{:S(2)}, u32[]{:S(2)}) %collective-permute-start.47) | collective-permute-done | bytes 1048608 | tf_op jit(solution)/shard_map/ppermute | solution.py:40
  512.3 7.8 %collective-permute-done.49 = bf16[2,8,40,384]{3,2,1,0:T(8,128)(2,1)S(1)} collective-permute-done((bf16[2,8,40,384]{3,2,1,0:T(8,128)(2,1)S(1)}, bf16[2,8,40,384]{3,2,1,0:T(8,128)(2,1)S(1)}, u32[]{:S(2)}, u32[]{:S(2)}) %collective-permute-start.49) | collective-permute-done | bytes 491552 | tf_op jit(solution)/shard_map/ppermute | solution.py:40
  524.2 8.8 %collective-permute-done.60 = bf16[64,1024]{1,0:T(8,128)(2,1)S(1)} collective-permute-done((bf16[64,1024]{1,0:T(8,128)(2,1)S(1)}, bf16[64,1024]{1,0:T(8,128)(2,1)S(1)}, u32[]{:S(2)}, u32[]{:S(2)}) %collective-permute-start.60) | collective-permute-done | bytes 131104 | tf_op jit(solution)/shard_map/ppermute | solution.py:40
  548.5 4.0 collective-permute-done.56
  (539 shorter events, 268.7 us)
Async XLA Ops:
  7.2 203.4 %all-gather.3.cloned.1.call-start = ((), (), s32[]{:S(2)}) async-start(), calls=%async_computation | async-start | bytes 19464192 | tf_op jit(solution)/shard_map/all_gather | solution.py:589
  15.5 20.3 %collective-permute-start.8 = (bf16[1,256,1024]{2,1,0:T(8,128)(2,1)S(1)}, bf16[1,256,1024]{2,1,0:T(8,128)(2,1)S(1)}, u32[]{:S(2)}, u32[]{:S(2)}) collective-permute-start(bf16[1,256,1024]{2,1,0:T(8,128)(2,1)S(1)} %get-tuple-element.231), channel_id=1, source_target_pairs={{0,4},{1,5},{2,6},{3,7},{4,0},{5,1},{6,2},{7,3},{8,12},{9,13},{10,... | collective-permute-start | bytes 1572872 | tf_op jit(solution)/shard_map/ppermute | solution.py:40
  36.8 28.9 %collective-permute-start.9 = (bf16[2,256,1024]{2,1,0:T(8,128)(2,1)}, bf16[2,256,1024]{2,1,0:T(8,128)(2,1)}, u32[]{:S(2)}, u32[]{:S(2)}) collective-permute-start(bf16[2,256,1024]{2,1,0:T(8,128)(2,1)} %pad_maximum_fusion.16), channel_id=1, source_target_pairs={{0,2},{1,3},{2,0},{3,1},{4,6},{5,7},{6,4},{7,5},{8,10},{9,11},{10,... | collective-permute-start | bytes 3145736 | tf_op jit(solution)/shard_map/ppermute | solution.py:40
  38.4 27.3 %collective-permute-start.1 = (bf16[2,256,1024]{2,1,0:T(8,128)(2,1)}, bf16[2,256,1024]{2,1,0:T(8,128)(2,1)S(1)}, u32[]{:S(2)}, u32[]{:S(2)}) collective-permute-start(bf16[2,256,1024]{2,1,0:T(8,128)(2,1)} %pad_maximum_fusion.15), channel_id=1, source_target_pairs={{0,4},{1,5},{2,6},{3,7},{4,0},{5,1},{6,2},{7,3},{8,12},{9,13},{10,... | collective-permute-start | bytes 3145736 | tf_op jit(solution)/shard_map/ppermute | solution.py:40
  100.6 30.0 %collective-permute-start.11 = (bf16[2,576,256]{2,1,0:T(8,128)(2,1)}, bf16[2,576,256]{2,1,0:T(8,128)(2,1)S(1)}, u32[]{:S(2)}, u32[]{:S(2)}) collective-permute-start(bf16[2,576,256]{2,1,0:T(8,128)(2,1)} %fusion.59), channel_id=1, source_target_pairs={{0,8},{1,9},{2,10},{3,11},{4,12},{5,13},{6,14},{7,15},{8,16},{9,17... | collective-permute-start | bytes 1769480 | tf_op jit(solution)/shard_map/ppermute | solution.py:46
  104.3 33.2 %collective-permute-start.12 = (bf16[2,576,256]{2,1,0:T(8,128)(2,1)S(1)}, bf16[2,576,256]{2,1,0:T(8,128)(2,1)S(1)}, u32[]{:S(2)}, u32[]{:S(2)}) collective-permute-start(bf16[2,576,256]{2,1,0:T(8,128)(2,1)S(1)} %fusion.57), channel_id=1, source_target_pairs={{8,0},{9,1},{10,2},{11,3},{12,4},{13,5},{14,6},{15,7},{16,8},{17,9... | collective-permute-start | bytes 1769480 | tf_op jit(solution)/shard_map/ppermute | solution.py:46
  170.1 23.1 %collective-permute-start.19 = (bf16[2,256,128]{2,1,0:T(8,128)(2,1)S(1)}, bf16[2,256,128]{2,1,0:T(8,128)(2,1)S(1)}, u32[]{:S(2)}, u32[]{:S(2)}) collective-permute-start(bf16[2,256,128]{2,1,0:T(8,128)(2,1)S(1)} %get-tuple-element.223), channel_id=1, source_target_pairs={{0,7},{1,6},{2,5},{3,4},{4,3},{5,2},{6,1},{7,0},{8,15},{9,14},{10,... | collective-permute-start | bytes 393224 | tf_op jit(solution)/shard_map/ppermute | solution.py:40
  172.5 20.6 %collective-permute-start.18 = (bf16[2,256,128]{2,1,0:T(8,128)(2,1)S(1)}, bf16[2,256,128]{2,1,0:T(8,128)(2,1)S(1)}, u32[]{:S(2)}, u32[]{:S(2)}) collective-permute-start(bf16[2,256,128]{2,1,0:T(8,128)(2,1)S(1)} %get-tuple-element.224), channel_id=1, source_target_pairs={{0,6},{1,7},{2,4},{3,5},{4,2},{5,3},{6,0},{7,1},{8,14},{9,15},{10,... | collective-permute-start | bytes 393224 | tf_op jit(solution)/shard_map/ppermute | solution.py:40
  173.1 20.0 %collective-permute-start.17 = (bf16[2,256,128]{2,1,0:T(8,128)(2,1)S(1)}, bf16[2,256,128]{2,1,0:T(8,128)(2,1)S(1)}, u32[]{:S(2)}, u32[]{:S(2)}) collective-permute-start(bf16[2,256,128]{2,1,0:T(8,128)(2,1)S(1)} %get-tuple-element.225), channel_id=1, source_target_pairs={{0,5},{1,4},{2,7},{3,6},{4,1},{5,0},{6,3},{7,2},{8,13},{9,12},{10,... | collective-permute-start | bytes 393224 | tf_op jit(solution)/shard_map/ppermute | solution.py:40
  284.3 27.1 %collective-permute-start.22 = (bf16[2,2,2,2,80,1024]{5,4,3,2,1,0:T(8,128)(2,1)S(1)}, bf16[2,2,2,2,80,1024]{5,4,3,2,1,0:T(8,128)(2,1)S(1)}, u32[]{:S(2)}, u32[]{:S(2)}) collective-permute-start(bf16[2,2,2,2,80,1024]{5,4,3,2,1,0:T(8,128)(2,1)S(1)} %pad_maximum_fusion.1), channel_id=1, source_target_pairs={{0,1},{1,0},{2,3},{3,2},{4,5},{5,4},{6,7},{7,6},{8,9},{9,8},{10,11... | collective-permute-start | bytes 7864328 | tf_op jit(solution)/shard_map/ppermute | solution.py:40
  284.7 26.8 %collective-permute-start.30 = (bf16[2,2,2,2,80,1024]{5,4,0,1,3,2:T(8,128)(2,1)S(1)}, bf16[2,2,2,2,80,1024]{5,4,0,1,3,2:T(8,128)(2,1)S(1)}, u32[]{:S(2)}, u32[]{:S(2)}) collective-permute-start(bf16[2,2,2,2,80,1024]{5,4,0,1,3,2:T(8,128)(2,1)S(1)} %copy.185), channel_id=1, source_target_pairs={{0,1},{1,0},{2,3},{3,2},{4,5},{5,4},{6,7},{7,6},{8,9},{9,8},{10,11... | collective-permute-start | bytes 7864328 | tf_op jit(solution)/shard_map/ppermute | solution.py:40
  308.7 34.0 %collective-permute-start.34 = (bf16[2,2,2,64,1024]{4,3,0,2,1:T(8,128)(2,1)}, bf16[2,2,2,64,1024]{4,3,0,2,1:T(8,128)(2,1)}, u32[]{:S(2)}, u32[]{:S(2)}) collective-permute-start(bf16[2,2,2,64,1024]{4,3,0,2,1:T(8,128)(2,1)} %get-tuple-element.152), channel_id=1, source_target_pairs={{0,8},{1,9},{2,10},{3,11},{4,12},{5,13},{6,14},{7,15},{8,0},{9,1},... | collective-permute-start | bytes 3145736 | tf_op jit(solution)/shard_map/ppermute | solution.py:40
  315.1 44.6 %collective-permute-start.32 = (bf16[2,2,2,80,1024]{4,3,0,2,1:T(8,128)(2,1)}, bf16[2,2,2,80,1024]{4,3,0,2,1:T(8,128)(2,1)}, u32[]{:S(2)}, u32[]{:S(2)}) collective-permute-start(bf16[2,2,2,80,1024]{4,3,0,2,1:T(8,128)(2,1)} %copy.166), channel_id=1, source_target_pairs={{0,4},{1,5},{2,6},{3,7},{4,0},{5,1},{6,2},{7,3},{8,12},{9,13},{10,... | collective-permute-start | bytes 3932168 | tf_op jit(solution)/shard_map/ppermute | solution.py:40
  317.0 42.6 %collective-permute-start.31 = (bf16[2,2,2,80,1024]{4,3,0,1,2:T(8,128)(2,1)}, bf16[2,2,2,80,1024]{4,3,0,1,2:T(8,128)(2,1)}, u32[]{:S(2)}, u32[]{:S(2)}) collective-permute-start(bf16[2,2,2,80,1024]{4,3,0,1,2:T(8,128)(2,1)} %fusion.28), channel_id=1, source_target_pairs={{0,2},{1,3},{2,0},{3,1},{4,6},{5,7},{6,4},{7,5},{8,10},{9,11},{10,... | collective-permute-start | bytes 3932168 | tf_op jit(solution)/shard_map/ppermute | solution.py:40
  318.4 39.1 %collective-permute-start.33 = (bf16[2,2,2,64,1024]{4,3,0,1,2:T(8,128)(2,1)}, bf16[2,2,2,64,1024]{4,3,0,1,2:T(8,128)(2,1)}, u32[]{:S(2)}, u32[]{:S(2)}) collective-permute-start(bf16[2,2,2,64,1024]{4,3,0,1,2:T(8,128)(2,1)} %fusion.34), channel_id=1, source_target_pairs={{0,8},{1,9},{2,10},{3,11},{4,12},{5,13},{6,14},{7,15},{8,0},{9,1},... | collective-permute-start | bytes 3145736 | tf_op jit(solution)/shard_map/ppermute | solution.py:40
  341.3 23.6 %collective-permute-start.36 = (bf16[768,256]{1,0:T(8,128)(2,1)}, bf16[768,256]{1,0:T(8,128)(2,1)S(1)}, u32[]{:S(2)}, u32[]{:S(2)}) collective-permute-start(bf16[768,256]{1,0:T(8,128)(2,1)} %get-tuple-element.73), channel_id=1, source_target_pairs={{8,0},{9,1},{10,2},{11,3},{12,4},{13,5},{14,6},{15,7},{16,8},{17,9... | collective-permute-start | bytes 1179656 | tf_op jit(solution)/shard_map/ppermute | solution.py:46
  342.7 22.0 %collective-permute-start.35 = (bf16[768,256]{1,0:T(8,128)(2,1)}, bf16[768,256]{1,0:T(8,128)(2,1)S(1)}, u32[]{:S(2)}, u32[]{:S(2)}) collective-permute-start(bf16[768,256]{1,0:T(8,128)(2,1)} %get-tuple-element.80), channel_id=1, source_target_pairs={{0,8},{1,9},{2,10},{3,11},{4,12},{5,13},{6,14},{7,15},{8,16},{9,17... | collective-permute-start | bytes 1179656 | tf_op jit(solution)/shard_map/ppermute | solution.py:46
  386.4 39.1 %collective-permute-start.42 = (bf16[2,2,64,1024]{3,2,0,1:T(8,128)(2,1)}, bf16[2,2,64,1024]{3,2,0,1:T(8,128)(2,1)}, u32[]{:S(2)}, u32[]{:S(2)}) collective-permute-start(bf16[2,2,64,1024]{3,2,0,1:T(8,128)(2,1)} %fusion.61), channel_id=1, source_target_pairs={{0,2},{1,3},{2,0},{3,1},{4,6},{5,7},{6,4},{7,5},{8,10},{9,11},{10,... | collective-permute-start | bytes 1572872 | tf_op jit(solution)/shard_map/ppermute | solution.py:40
  387.8 36.3 %collective-permute-start.43 = (bf16[2,2,64,1024]{3,2,1,0:T(8,128)(2,1)}, bf16[2,2,64,1024]{3,2,1,0:T(8,128)(2,1)}, u32[]{:S(2)}, u32[]{:S(2)}) collective-permute-start(bf16[2,2,64,1024]{3,2,1,0:T(8,128)(2,1)} %copy.175), channel_id=1, source_target_pairs={{0,4},{1,5},{2,6},{3,7},{4,0},{5,1},{6,2},{7,3},{8,12},{9,13},{10,... | collective-permute-start | bytes 1572872 | tf_op jit(solution)/shard_map/ppermute | solution.py:40
  389.4 36.1 %collective-permute-start.40 = (bf16[2,2,80,1024]{3,2,0,1:T(8,128)(2,1)}, bf16[2,2,80,1024]{3,2,0,1:T(8,128)(2,1)}, u32[]{:S(2)}, u32[]{:S(2)}) collective-permute-start(bf16[2,2,80,1024]{3,2,0,1:T(8,128)(2,1)} %fusion.51), channel_id=1, source_target_pairs={{0,4},{1,5},{2,6},{3,7},{4,0},{5,1},{6,2},{7,3},{8,12},{9,13},{10,... | collective-permute-start | bytes 1966088 | tf_op jit(solution)/shard_map/ppermute | solution.py:40
  390.7 34.8 %collective-permute-start.41 = (bf16[2,2,80,1024]{3,2,1,0:T(8,128)(2,1)}, bf16[2,2,80,1024]{3,2,1,0:T(8,128)(2,1)}, u32[]{:S(2)}, u32[]{:S(2)}) collective-permute-start(bf16[2,2,80,1024]{3,2,1,0:T(8,128)(2,1)} %copy.172), channel_id=1, source_target_pairs={{0,2},{1,3},{2,0},{3,1},{4,6},{5,7},{6,4},{7,5},{8,10},{9,11},{10,... | collective-permute-start | bytes 1966088 | tf_op jit(solution)/shard_map/ppermute | solution.py:40
  398.1 41.8 %collective-permute-start.38 = (bf16[2,256,1024]{2,1,0:T(8,128)(2,1)}, bf16[2,256,1024]{2,1,0:T(8,128)(2,1)}, u32[]{:S(2)}, u32[]{:S(2)}) collective-permute-start(bf16[2,256,1024]{2,1,0:T(8,128)(2,1)} %pad_maximum_fusion.17), channel_id=1, source_target_pairs={{0,2},{1,3},{2,0},{3,1},{4,6},{5,7},{6,4},{7,5},{8,10},{9,11},{10,... | collective-permute-start | bytes 3145736 | tf_op jit(solution)/shard_map/ppermute | solution.py:40
  456.2 47.6 %collective-permute-start.52 = (bf16[2,64,1024]{2,1,0:T(8,128)(2,1)}, bf16[2,64,1024]{2,1,0:T(8,128)(2,1)}, u32[]{:S(2)}, u32[]{:S(2)}) collective-permute-start(bf16[2,64,1024]{2,1,0:T(8,128)(2,1)} %get-tuple-element.194), channel_id=1, source_target_pairs={{0,4},{1,5},{2,6},{3,7},{4,0},{5,1},{6,2},{7,3},{8,12},{9,13},{10,... | collective-permute-start | bytes 786440 | tf_op jit(solution)/shard_map/ppermute | solution.py:40
  457.0 46.2 %collective-permute-start.53 = (bf16[2,64,1024]{2,1,0:T(8,128)(2,1)}, bf16[2,64,1024]{2,1,0:T(8,128)(2,1)}, u32[]{:S(2)}, u32[]{:S(2)}) collective-permute-start(bf16[2,64,1024]{2,1,0:T(8,128)(2,1)} %get-tuple-element.192), channel_id=1, source_target_pairs={{0,2},{1,3},{2,0},{3,1},{4,6},{5,7},{6,4},{7,5},{8,10},{9,11},{10,... | collective-permute-start | bytes 786440 | tf_op jit(solution)/shard_map/ppermute | solution.py:40
  457.2 46.7 %collective-permute-start.50 = (bf16[2,80,1024]{2,1,0:T(8,128)(2,1)}, bf16[2,80,1024]{2,1,0:T(8,128)(2,1)}, u32[]{:S(2)}, u32[]{:S(2)}) collective-permute-start(bf16[2,80,1024]{2,1,0:T(8,128)(2,1)} %get-tuple-element.190), channel_id=1, source_target_pairs={{0,8},{1,9},{2,10},{3,11},{4,12},{5,13},{6,14},{7,15},{8,0},{9,1},... | collective-permute-start | bytes 983048 | tf_op jit(solution)/shard_map/ppermute | solution.py:40
  465.6 38.3 %collective-permute-start.51 = (bf16[2,80,1024]{2,1,0:T(8,128)(2,1)}, bf16[2,80,1024]{2,1,0:T(8,128)(2,1)}, u32[]{:S(2)}, u32[]{:S(2)}) collective-permute-start(bf16[2,80,1024]{2,1,0:T(8,128)(2,1)} %get-tuple-element.188), channel_id=1, source_target_pairs={{0,8},{1,9},{2,10},{3,11},{4,12},{5,13},{6,14},{7,15},{8,0},{9,1},... | collective-permute-start | bytes 983048 | tf_op jit(solution)/shard_map/ppermute | solution.py:40
  476.5 25.0 %collective-permute-start.47 = (bf16[2,256,1024]{2,1,0:T(8,128)(2,1)}, bf16[2,256,1024]{2,1,0:T(8,128)(2,1)}, u32[]{:S(2)}, u32[]{:S(2)}) collective-permute-start(bf16[2,256,1024]{2,1,0:T(8,128)(2,1)} %pad_maximum_fusion.18), channel_id=1, source_target_pairs={{0,4},{1,5},{2,6},{3,7},{4,0},{5,1},{6,2},{7,3},{8,12},{9,13},{10,... | collective-permute-start | bytes 3145736 | tf_op jit(solution)/shard_map/ppermute | solution.py:40
  503.1 40.5 %collective-permute-start.48 = (bf16[1,256,1024]{2,1,0:T(8,128)(2,1)S(1)}, bf16[1,256,1024]{2,1,0:T(8,128)(2,1)S(1)}, u32[]{:S(2)}, u32[]{:S(2)}) collective-permute-start(bf16[1,256,1024]{2,1,0:T(8,128)(2,1)S(1)} %add_convert_fusion.11), channel_id=1, source_target_pairs={{0,2},{1,3},{2,0},{3,1},{4,6},{5,7},{6,4},{7,5},{8,10},{9,11},{10,... | collective-permute-start | bytes 1572872 | tf_op jit(solution)/shard_map/ppermute | solution.py:40
  507.3 25.6 %collective-permute-start.60 = (bf16[64,1024]{1,0:T(8,128)(2,1)S(1)}, bf16[64,1024]{1,0:T(8,128)(2,1)S(1)}, u32[]{:S(2)}, u32[]{:S(2)}) collective-permute-start(bf16[64,1024]{1,0:T(8,128)(2,1)S(1)} %fusion.94), channel_id=1, source_target_pairs={{0,16},{1,17},{2,18},{3,19},{4,20},{5,21},{6,22},{7,23},{8,24},{9,... | collective-permute-start | bytes 393224 | tf_op jit(solution)/shard_map/ppermute | solution.py:40
  509.8 26.6 %collective-permute-start.59 = (bf16[80,1024]{1,0:T(8,128)(2,1)S(1)}, bf16[80,1024]{1,0:T(8,128)(2,1)S(1)}, u32[]{:S(2)}, u32[]{:S(2)}) collective-permute-start(bf16[80,1024]{1,0:T(8,128)(2,1)S(1)} %fusion.85), channel_id=1, source_target_pairs={{0,16},{1,17},{2,18},{3,19},{4,20},{5,21},{6,22},{7,23},{8,24},{9,... | collective-permute-start | bytes 491528 | tf_op jit(solution)/shard_map/ppermute | solution.py:40
  520.1 19.9 %collective-permute-start.58 = (bf16[80,1024]{1,0:T(8,128)(2,1)S(1)}, bf16[80,1024]{1,0:T(8,128)(2,1)S(1)}, u32[]{:S(2)}, u32[]{:S(2)}) collective-permute-start(bf16[80,1024]{1,0:T(8,128)(2,1)S(1)} %fusion.84), channel_id=1, source_target_pairs={{0,16},{1,17},{2,18},{3,19},{4,20},{5,21},{6,22},{7,23},{8,24},{9,... | collective-permute-start | bytes 491528 | tf_op jit(solution)/shard_map/ppermute | solution.py:40
  520.2 23.3 %collective-permute-start.54 = (bf16[1,8,40,384]{3,2,1,0:T(8,128)(2,1)S(1)}, bf16[1,8,40,384]{3,2,1,0:T(8,128)(2,1)S(1)}, u32[]{:S(2)}, u32[]{:S(2)}) collective-permute-start(bf16[1,8,40,384]{3,2,1,0:T(8,128)(2,1)S(1)} %slice_bitcast_fusion.17), channel_id=1, source_target_pairs={{0,16},{1,17},{2,18},{3,19},{4,20},{5,21},{6,22},{7,23},{8,24},{9,... | collective-permute-start | bytes 737288 | tf_op jit(solution)/shard_map/ppermute | solution.py:40
  (116 other events, 927.9 us)
Sparse Core Ops, SparseCore 0:
  65.9 144.6 all-gather.2
